TPU v7x, 32 devices: a whole 2x2x4 slice. The times are simulated.
32 devices in a mesh: dp: 4 (over y, x), ctx: 8 (over z, core).
Axes of the slice: x: 2, y: 2, z: 4, core: 2. Of those that a mesh axis runs over, the one named last changes fastest.
Arguments:
- inputs: float32 [4, 1024, 1088], P('dp', 'ctx'), may hold values from -6 to 6
- out_grad: float32 [4, 1024, 1088], P('dp', 'ctx'), may hold values from -6 to 6
- pair_blocks: int32 [8, 2], replicated, may hold values from 0 to 15, as said below
- triple_weight: float32 [1088, 3264], P('ctx', 'dp')
- merge_weight: float32 [1088, 1088], P('ctx', 'dp'), may hold values from -0.75 to 0.75
- expand_weight: float32 [1088, 4352], P('ctx', 'dp'), may hold values from -0.1875 to 0.1875
- shrink_weight: float32 [4352, 1088], P('ctx', 'dp'), may hold values from -0.09375 to 0.09375
- vector_params: float32 [1088, 12], P('ctx', 'dp')
- triple_moment: float32 [1088, 3264], P('ctx', 'dp'), may hold values from -24 to 24
- merge_moment: float32 [1088, 1088], P('ctx', 'dp'), may hold values from -6 to 6
- expand_moment: float32 [1088, 4352], P('ctx', 'dp'), may hold values from -6 to 6
- shrink_moment: float32 [4352, 1088], P('ctx', 'dp'), may hold values from -6 to 6
- vector_moment: float32 [1088, 12], P('ctx', 'dp'), may hold values from -112 to 112
- triple_square: float32 [1088, 3264], P('ctx', 'dp'), may hold values from 24.576 to 245.76
- merge_square: float32 [1088, 1088], P('ctx', 'dp'), may hold values from 8.192 to 81.92
- expand_square: float32 [1088, 4352], P('ctx', 'dp'), may hold values from 8.192 to 81.92
- shrink_square: float32 [4352, 1088], P('ctx', 'dp'), may hold values from 8.192 to 81.92
- vector_square: float32 [1088, 12], P('ctx', 'dp'), may hold values from 204.8 to 2048
Outputs:
- block_output: float32 [4, 1024, 1088], P('dp', 'ctx')
- input_grad: float32 [4, 1024, 1088], P('dp', 'ctx')
- triple_grad: float32 [1088, 3264], P('ctx', 'dp')
- merge_grad: float32 [1088, 1088], P('ctx', 'dp')
- expand_grad: float32 [1088, 4352], P('ctx', 'dp')
- shrink_grad: float32 [4352, 1088], P('ctx', 'dp')
- vector_grad: float32 [1088, 12], P('ctx', 'dp')
- triple_new: float32 [1088, 3264], P('ctx', 'dp')
- merge_new: float32 [1088, 1088], P('ctx', 'dp')
- expand_new: float32 [1088, 4352], P('ctx', 'dp')
- shrink_new: float32 [4352, 1088], P('ctx', 'dp')
- vector_new: float32 [1088, 12], P('ctx', 'dp')
- triple_moment_new: float32 [1088, 3264], P('ctx', 'dp')
- merge_moment_new: float32 [1088, 1088], P('ctx', 'dp')
- expand_moment_new: float32 [1088, 4352], P('ctx', 'dp')
- shrink_moment_new: float32 [4352, 1088], P('ctx', 'dp')
- vector_moment_new: float32 [1088, 12], P('ctx', 'dp')
- triple_square_new: float32 [1088, 3264], P('ctx', 'dp')
- merge_square_new: float32 [1088, 1088], P('ctx', 'dp')
- expand_square_new: float32 [1088, 4352], P('ctx', 'dp')
- shrink_square_new: float32 [4352, 1088], P('ctx', 'dp')
- vector_square_new: float32 [1088, 12], P('ctx', 'dp')
Inputs may be any that keep to these rules, and one draw needn't show every extreme that they name: `pair_blocks`: row c names the two blocks of 64 positions that stand in stored rows c * 2 * 64 onward: first a block p, then 2 * 8 - 1 - p; each of the 16 blocks is named once.
All inputs are finite; a program needn't handle non-finite values.
Results may differ from a plain program's by a relative error of at most 0.011.
Values may be sent and summed in bfloat16 or wider, within the bound.
A program may use at most 256 MiB of HBM per device.

v0:
```python
import jax
import jax.numpy as jnp
from jax import lax
from jax.sharding import PartitionSpec as P

D = 1088
H = 17
HD = 64
BLK = 64


norm_eps = 1e-05
beta_first = 0.9
beta_second = 0.95
learn_rate = 0.01
decay_rate = 0.1
adam_eps = 1e-08
adam_steps = 4
gelu_coef = 0.7978845608028654
masked_score = -1e30


def layer_norm(values):
    center = jnp.mean(values, axis=-1, keepdims=True)
    shifted = values - center
    inverse = lax.rsqrt(jnp.mean(shifted * shifted, axis=-1, keepdims=True) + norm_eps)
    return (shifted * inverse, inverse)


def norm_back(incoming, normed, inverse, gain_vec):
    scaled = incoming * gain_vec
    return inverse * (
        scaled
        - jnp.mean(scaled, axis=-1, keepdims=True)
        - normed * jnp.mean(scaled * normed, axis=-1, keepdims=True)
    )


def gelu_value(values):
    inside = gelu_coef * (values + 0.044715 * values * values * values)
    return 0.5 * values * (1.0 + jnp.tanh(inside))


def gelu_slope(values):
    inside = gelu_coef * (values + 0.044715 * values * values * values)
    tangent = jnp.tanh(inside)
    return 0.5 * (1.0 + tangent) + 0.5 * values * (1.0 - tangent * tangent) * gelu_coef * (
        1.0 + 3.0 * 0.044715 * values * values
    )


def adam_update(weight, gradient, moment, square, decayed):
    moment_new = beta_first * moment + (1.0 - beta_first) * gradient
    square_new = beta_second * square + (1.0 - beta_second) * gradient * gradient
    first_fix = 1.0 - beta_first**adam_steps
    second_fix = 1.0 - beta_second**adam_steps
    direction = moment_new / first_fix / (jnp.sqrt(square_new / second_fix) + adam_eps)
    if decayed:
        direction = direction + decay_rate * weight
    return (weight - learn_rate * direction, moment_new, square_new)


def split_heads(values):
    return values.reshape(values.shape[0], H, HD).transpose(1, 0, 2)


def join_heads(values):
    return values.transpose(1, 0, 2).reshape(values.shape[1], H * HD)


def gather_params(first_part, second_part, third_part, fourth_part, fifth_part):
    piece_one, piece_two, piece_three, piece_four, piece_five = (
        lax.all_gather(first_part, "ctx", axis=0, tiled=True),
        lax.all_gather(second_part, "ctx", axis=0, tiled=True),
        lax.all_gather(third_part, "ctx", axis=0, tiled=True),
        lax.all_gather(fourth_part, "ctx", axis=0, tiled=True),
        lax.all_gather(fifth_part, "ctx", axis=0, tiled=True),
    )
    return (
        lax.all_gather(piece_one, "dp", axis=1, tiled=True),
        lax.all_gather(piece_two, "dp", axis=1, tiled=True),
        lax.all_gather(piece_three, "dp", axis=1, tiled=True),
        lax.all_gather(piece_four, "dp", axis=1, tiled=True),
        lax.all_gather(piece_five, "dp", axis=1, tiled=True),
    )


def reduce_grads(first_part, second_part, third_part, fourth_part, fifth_part):
    piece_one, piece_two, piece_three, piece_four, piece_five = (
        lax.psum_scatter(first_part, "ctx", scatter_dimension=0, tiled=True),
        lax.psum_scatter(second_part, "ctx", scatter_dimension=0, tiled=True),
        lax.psum_scatter(third_part, "ctx", scatter_dimension=0, tiled=True),
        lax.psum_scatter(fourth_part, "ctx", scatter_dimension=0, tiled=True),
        lax.psum_scatter(fifth_part, "ctx", scatter_dimension=0, tiled=True),
    )
    return (
        lax.psum_scatter(piece_one, "dp", scatter_dimension=1, tiled=True),
        lax.psum_scatter(piece_two, "dp", scatter_dimension=1, tiled=True),
        lax.psum_scatter(piece_three, "dp", scatter_dimension=1, tiled=True),
        lax.psum_scatter(piece_four, "dp", scatter_dimension=1, tiled=True),
        lax.psum_scatter(piece_five, "dp", scatter_dimension=1, tiled=True),
    )


def gather_keys(key_rows, value_rows):
    return (
        lax.all_gather(key_rows, "ctx", axis=0, tiled=True),
        lax.all_gather(value_rows, "ctx", axis=0, tiled=True),
    )


def local(
    inputs,
    out_grad,
    pair_blocks,
    triple_weight,
    merge_weight,
    expand_weight,
    shrink_weight,
    vector_params,
    triple_moment,
    merge_moment,
    expand_moment,
    shrink_moment,
    vector_moment,
    triple_square,
    merge_square,
    expand_square,
    shrink_square,
    vector_square,
):
    rows_here = inputs.shape[1]
    stream = inputs[0]
    cotangent = out_grad[0]
    offsets = jnp.arange(BLK, dtype=jnp.int32)
    all_positions = (pair_blocks.reshape(-1)[:, None] * BLK + offsets[None, :]).reshape(-1)
    query_positions = lax.dynamic_slice_in_dim(
        all_positions, lax.axis_index("ctx") * rows_here, rows_here
    )
    allowed = query_positions[:, None] >= all_positions[None, :]
    score_scale = HD ** (-0.5)
    copy_triple = triple_weight.astype(jnp.bfloat16)
    copy_merge = merge_weight.astype(jnp.bfloat16)
    copy_expand = expand_weight.astype(jnp.bfloat16)
    copy_shrink = shrink_weight.astype(jnp.bfloat16)
    copy_vector = vector_params.astype(jnp.bfloat16)
    w_triple, w_merge, w_expand, w_shrink, w_vector = gather_params(
        copy_triple, copy_merge, copy_expand, copy_shrink, copy_vector
    )
    vectors = w_vector.astype(jnp.float32)
    gain_one = vectors[:, 0]
    shift_one = vectors[:, 1]
    query_bias = vectors[:, 2]
    value_bias = vectors[:, 3]
    merge_bias = vectors[:, 4]
    gain_two = vectors[:, 5]
    shift_two = vectors[:, 6]
    shrink_bias = vectors[:, 7]
    expand_bias = vectors[:, 8:12].T.reshape(-1)
    normed_one, inverse_one = layer_norm(stream)
    act_one = (normed_one * gain_one + shift_one).astype(jnp.bfloat16)
    triple = jnp.dot(act_one, w_triple, preferred_element_type=jnp.float32)
    query_b = (triple[:, :D] + query_bias).astype(jnp.bfloat16)
    key_b = triple[:, D : 2 * D].astype(jnp.bfloat16)
    value_b = (triple[:, 2 * D :] + value_bias).astype(jnp.bfloat16)
    keys_all, values_all = gather_keys(key_b, value_b)

    def head_scores(query_h, key_h):
        scores = (
            lax.dot_general(
                query_h, key_h, (((1,), (1,)), ((), ())), preferred_element_type=jnp.float32
            )
            * score_scale
        )
        return jnp.where(allowed, scores, masked_score)

    def head_forward(operands):
        query_h, key_h, value_h = operands
        scores = head_scores(query_h, key_h)
        row_max = jnp.max(scores, axis=1, keepdims=True)
        log_total = row_max + jnp.log(jnp.sum(jnp.exp(scores - row_max), axis=1, keepdims=True))
        probs_b = jnp.exp(scores - log_total).astype(jnp.bfloat16)
        attended = jnp.dot(probs_b, value_h, preferred_element_type=jnp.float32)
        return (attended.astype(jnp.bfloat16), log_total[:, 0])

    heads_query = split_heads(query_b)
    heads_key = split_heads(keys_all)
    heads_value = split_heads(values_all)
    heads_out, heads_total = lax.map(head_forward, (heads_query, heads_key, heads_value))
    attended_b = join_heads(heads_out)
    middle = stream + jnp.dot(attended_b, w_merge, preferred_element_type=jnp.float32) + merge_bias
    normed_two, inverse_two = layer_norm(middle)
    act_two = (normed_two * gain_two + shift_two).astype(jnp.bfloat16)
    pre_act = jnp.dot(act_two, w_expand, preferred_element_type=jnp.float32) + expand_bias
    hidden_b = gelu_value(pre_act).astype(jnp.bfloat16)
    block_out = (
        middle + jnp.dot(hidden_b, w_shrink, preferred_element_type=jnp.float32) + shrink_bias
    )
    back_triple, back_merge, back_expand, back_shrink, unused_vector = gather_params(
        copy_triple, copy_merge, copy_expand, copy_shrink, copy_vector
    )
    keys_again, values_again = gather_keys(key_b, value_b)
    back_key = split_heads(keys_again)
    back_value = split_heads(values_again)
    cotangent_b = cotangent.astype(jnp.bfloat16)
    shrink_local = jnp.dot(hidden_b.T, cotangent_b, preferred_element_type=jnp.float32)
    shrink_bias_grad = jnp.sum(cotangent, axis=0)
    dpre = jnp.dot(cotangent_b, back_shrink.T, preferred_element_type=jnp.float32) * gelu_slope(
        pre_act
    )
    dpre_b = dpre.astype(jnp.bfloat16)
    expand_local = jnp.dot(act_two.T, dpre_b, preferred_element_type=jnp.float32)
    expand_bias_grad = jnp.sum(dpre, axis=0)
    dact_two = jnp.dot(dpre_b, back_expand.T, preferred_element_type=jnp.float32)
    gain_two_grad = jnp.sum(dact_two * normed_two, axis=0)
    shift_two_grad = jnp.sum(dact_two, axis=0)
    dmiddle = cotangent + norm_back(dact_two, normed_two, inverse_two, gain_two)
    dmiddle_b = dmiddle.astype(jnp.bfloat16)
    merge_local = jnp.dot(attended_b.T, dmiddle_b, preferred_element_type=jnp.float32)
    merge_bias_grad = jnp.sum(dmiddle, axis=0)
    dattended_b = jnp.dot(dmiddle_b, back_merge.T, preferred_element_type=jnp.float32).astype(
        jnp.bfloat16
    )

    def head_backward(operands):
        query_h, key_h, value_h, out_h, dout_h, log_total = operands
        scores = head_scores(query_h, key_h)
        probs = jnp.exp(scores - log_total[:, None])
        probs_b = probs.astype(jnp.bfloat16)
        delta = jnp.sum(
            dout_h.astype(jnp.float32) * out_h.astype(jnp.float32), axis=1, keepdims=True
        )
        dprobs = lax.dot_general(
            dout_h, value_h, (((1,), (1,)), ((), ())), preferred_element_type=jnp.float32
        )
        dscores_b = (probs * (dprobs - delta) * score_scale).astype(jnp.bfloat16)
        dquery_h = jnp.dot(dscores_b, key_h, preferred_element_type=jnp.float32)
        dkey_h = lax.dot_general(
            dscores_b, query_h, (((0,), (0,)), ((), ())), preferred_element_type=jnp.float32
        )
        dvalue_h = lax.dot_general(
            probs_b, dout_h, (((0,), (0,)), ((), ())), preferred_element_type=jnp.float32
        )
        return (dquery_h, dkey_h, dvalue_h)

    dquery_heads, dkey_heads, dvalue_heads = lax.map(
        head_backward,
        (heads_query, back_key, back_value, heads_out, split_heads(dattended_b), heads_total),
    )
    dquery = join_heads(dquery_heads)
    dkey_rows, dvalue_rows = (
        lax.psum_scatter(join_heads(dkey_heads), "ctx", scatter_dimension=0, tiled=True),
        lax.psum_scatter(join_heads(dvalue_heads), "ctx", scatter_dimension=0, tiled=True),
    )
    dtriple_b = jnp.concatenate([dquery, dkey_rows, dvalue_rows], axis=1).astype(jnp.bfloat16)
    triple_local = jnp.dot(act_one.T, dtriple_b, preferred_element_type=jnp.float32)
    query_bias_grad = jnp.sum(dquery, axis=0)
    value_bias_grad = jnp.sum(dvalue_rows, axis=0)
    dact_one = jnp.dot(dtriple_b, back_triple.T, preferred_element_type=jnp.float32)
    gain_one_grad = jnp.sum(dact_one * normed_one, axis=0)
    shift_one_grad = jnp.sum(dact_one, axis=0)
    input_rows = dmiddle + norm_back(dact_one, normed_one, inverse_one, gain_one)
    vector_local = jnp.concatenate(
        [
            jnp.stack(
                [
                    gain_one_grad,
                    shift_one_grad,
                    query_bias_grad,
                    value_bias_grad,
                    merge_bias_grad,
                    gain_two_grad,
                    shift_two_grad,
                    shrink_bias_grad,
                ],
                axis=1,
            ),
            expand_bias_grad.reshape(4, D).T,
        ],
        axis=1,
    )
    triple_grad, merge_grad, expand_grad, shrink_grad, vector_grad = reduce_grads(
        triple_local, merge_local, expand_local, shrink_local, vector_local
    )
    triple_new, triple_moment_new, triple_square_new = adam_update(
        triple_weight, triple_grad, triple_moment, triple_square, True
    )
    merge_new, merge_moment_new, merge_square_new = adam_update(
        merge_weight, merge_grad, merge_moment, merge_square, True
    )
    expand_new, expand_moment_new, expand_square_new = adam_update(
        expand_weight, expand_grad, expand_moment, expand_square, True
    )
    shrink_new, shrink_moment_new, shrink_square_new = adam_update(
        shrink_weight, shrink_grad, shrink_moment, shrink_square, True
    )
    vector_new, vector_moment_new, vector_square_new = adam_update(
        vector_params, vector_grad, vector_moment, vector_square, False
    )
    return (
        block_out[None],
        input_rows[None],
        triple_grad,
        merge_grad,
        expand_grad,
        shrink_grad,
        vector_grad,
        triple_new,
        merge_new,
        expand_new,
        shrink_new,
        vector_new,
        triple_moment_new,
        merge_moment_new,
        expand_moment_new,
        shrink_moment_new,
        vector_moment_new,
        triple_square_new,
        merge_square_new,
        expand_square_new,
        shrink_square_new,
        vector_square_new,
    )


def solution(mesh):
    in_specs = (
        P("dp", "ctx", None),
        P("dp", "ctx", None),
        P(),
        P("ctx", "dp"),
        P("ctx", "dp"),
        P("ctx", "dp"),
        P("ctx", "dp"),
        P("ctx", "dp"),
        P("ctx", "dp"),
        P("ctx", "dp"),
        P("ctx", "dp"),
        P("ctx", "dp"),
        P("ctx", "dp"),
        P("ctx", "dp"),
        P("ctx", "dp"),
        P("ctx", "dp"),
        P("ctx", "dp"),
        P("ctx", "dp"),
    )
    out_specs = (
        P("dp", "ctx", None),
        P("dp", "ctx", None),
        P("ctx", "dp"),
        P("ctx", "dp"),
        P("ctx", "dp"),
        P("ctx", "dp"),
        P("ctx", "dp"),
        P("ctx", "dp"),
        P("ctx", "dp"),
        P("ctx", "dp"),
        P("ctx", "dp"),
        P("ctx", "dp"),
        P("ctx", "dp"),
        P("ctx", "dp"),
        P("ctx", "dp"),
        P("ctx", "dp"),
        P("ctx", "dp"),
        P("ctx", "dp"),
        P("ctx", "dp"),
        P("ctx", "dp"),
        P("ctx", "dp"),
        P("ctx", "dp"),
    )
    return jax.shard_map(local, mesh=mesh, in_specs=in_specs, out_specs=out_specs, check_vma=False)
```

profile of v0, /device:TPU:0, one launch (start us, length us, event | category | flops | bytes accessed | tf_op | source)
XLA Modules:
  0.0 1586.5 jit_solution(11072138455714467575)
XLA Ops:
  9.1 31.8 %all-gather.13.cloned.1.call-done = bf16[1088,816]{1,0:T(8,128)(2,1)} async-done(((bf16[136,816]{1,0:T(8,128)(2,1)}), bf16[1088,816]{1,0:T(8,128)(2,1)}) %all-gather.13.cloned.1.call-update) | async-done | bytes 1775632 | tf_op jit(solution)/shard_map/all_gather | solution.py:73
  46.9 12.8 all-gather
  59.8 8.8 all-gather.1
  69.6 55.4 %all-gather.15.cloned.1.call-done = bf16[1088,3264]{0,1:T(8,128)(2,1)} async-done(((bf16[1088,816]{0,1:T(8,128)(2,1)}), bf16[1088,3264]{0,1:T(8,128)(2,1)}) %all-gather.15.cloned.1.call-update) | async-done | bytes 7102480 | tf_op jit(solution)/shard_map/all_gather | solution.py:80
  125.0 5.4 fusion.75
  132.6 21.3 %all_gather.52 = bf16[1088,272]{1,0:T(8,128)(2,1)S(1)} all-gather(bf16[136,272]{1,0:T(8,128)(2,1)S(1)} %convert_element_type.74), channel_id=1, replica_groups=mesh['dp'=4,'ctx'=8] {'ctx'}, dimensions={0}, use_global_device_ids=true | all-gather | bytes 665856 | tf_op jit(solution)/shard_map/all_gather | solution.py:74
  155.0 11.0 all-gather.23.cloned.1.call-done
  173.4 28.5 %all-gather.29.cloned.1.call-done = bf16[8,544,272]{1,2,0:T(8,128)(2,1)} async-done(((bf16[1,544,272]{1,2,0:T(8,128)(2,1)}), bf16[8,544,272]{1,2,0:T(8,128)(2,1)}) %all-gather.29.cloned.1.call-update) | async-done | bytes 2367504 | tf_op jit(solution)/shard_map/all_gather | solution.py:76
  208.6 26.0 %all-gather.17.cloned.1.call-done = bf16[1024,1088]{0,1:T(8,128)(2,1)} async-done(((bf16[128,1088]{0,1:T(8,128)(2,1)}), bf16[1024,1088]{0,1:T(8,128)(2,1)}) %all-gather.17.cloned.1.call-update) | async-done | bytes 2228240 | tf_op jit(solution)/shard_map/all_gather | solution.py:107
  239.9 27.4 %all-gather.19.cloned.1.call-done = bf16[1024,1088]{0,1:T(8,128)(2,1)} async-done(((bf16[128,1088]{0,1:T(8,128)(2,1)}), bf16[1024,1088]{0,1:T(8,128)(2,1)}) %all-gather.19.cloned.1.call-update) | async-done | bytes 2228240 | tf_op jit(solution)/shard_map/all_gather | solution.py:108
  272.6 69.6 %while.28 = (s32[]{:T(128)}, bf16[17,128,64]{1,2,0:T(8,128)(2,1)S(1)}, f32[17,128]{1,0:T(8,128)}, bf16[17,128,64]{2,1,0:T(8,128)(2,1)S(1)}, bf16[17,1024,64]{2,1...) while((s32[]{:T(128)}, ...), condition=%wide.region_5.6_spmd.clone, body=%wide.region_2.5_spmd.clone.sunk | while | flops 34611072 | bytes 2157681 | solution.py:189
  346.3 64.1 %all-gather.25.cloned.1.call-done = bf16[1088,4352]{0,1:T(8,128)(2,1)} async-done(((bf16[1088,1088]{0,1:T(8,128)(2,1)}), bf16[1088,4352]{0,1:T(8,128)(2,1)}) %all-gather.25.cloned.1.call-update) | async-done | bytes 9469968 | tf_op jit(solution)/shard_map/all_gather | solution.py:82
  410.4 7.3 convolution_add_fusion
  417.6 91.1 %all-gather.27.cloned.1.call-done = bf16[4352,1088]{0,1:T(8,128)(2,1)} async-done(((bf16[4352,272]{0,1:T(8,128)(2,1)}), bf16[4352,1088]{0,1:T(8,128)(2,1)}) %all-gather.27.cloned.1.call-update) | async-done | bytes 9469968 | tf_op jit(solution)/shard_map/all_gather | solution.py:83
  508.8 7.5 fusion.87
  523.9 133.4 %while.29 = (s32[]{:T(128)}, f32[17,128,64]{1,2,0:T(8,128)}, f32[17,1024,64]{1,2,0:T(8,128)}, f32[17,1024,64]{1,2,0:T(8,128)}, bf16[17,128,64]{2,1,0:T(8,128)(2,...) while((s32[]{:T(128)}, f32[17,128,64]{1,2,0:T(8,128)}, ...), condition=%wide.region_12.13_spmd.clone, body=%wide.region_10.12_spmd.clone.sunk | while | flops 85098368 | bytes 3944593 | solution.py:246
  662.7 9.6 fusion.68
  674.2 35.6 %reduce-scatter.20.cloned.1.call-done = f32[128,1088]{0,1:T(8,128)} async-done(((f32[1024,1088]{0,1:T(8,128)}), f32[128,1088]{0,1:T(8,128)}) %reduce-scatter.20.cloned.1.call-update) | async-done | bytes 557072 | tf_op jit(solution)/shard_map/reduce_scatter | solution.py:252
  711.6 51.4 %reduce-scatter.22.cloned.1.call-done = f32[128,1088]{0,1:T(8,128)} async-done(((f32[1024,1088]{0,1:T(8,128)}), f32[128,1088]{0,1:T(8,128)}) %reduce-scatter.22.cloned.1.call-update) | async-done | bytes 557072 | tf_op jit(solution)/shard_map/reduce_scatter | solution.py:253
  765.9 8.5 fusion.65
  775.0 9.5 fusion.59
  784.6 37.1 %reduce-scatter.36.cloned.1.call-done = f32[136,1088]{1,0:T(8,128)} async-done(((f32[1088,1088]{1,0:T(8,128)}), f32[136,1088]{1,0:T(8,128)}) %reduce-scatter.36.cloned.1.call-update) | async-done | bytes 591888
  824.2 197.3 %reduce-scatter.28.cloned.1.call-done = f32[544,1088]{1,0:T(8,128)} async-done(((f32[4352,1088]{1,0:T(8,128)}), f32[544,1088]{1,0:T(8,128)}) %reduce-scatter.28.cloned.1.call-update) | async-done | bytes 2367504 | tf_op jit(solution)/shard_map/reduce_scatter | solution.py:93
  1021.6 147.7 %reduce-scatter.24.cloned.1.call-done = f32[136,3264]{1,0:T(8,128)} async-done(((f32[1088,3264]{1,0:T(8,128)}), f32[136,3264]{1,0:T(8,128)}) %reduce-scatter.24.cloned.1.call-update) | async-done | bytes 1775632 | tf_op jit(solution)/shard_map/reduce_scatter | solution.py:90
  1172.7 186.2 %reduce-scatter.26.cloned.1.call-done = f32[136,4352]{1,0:T(8,128)} async-done(((f32[1088,4352]{1,0:T(8,128)}), f32[136,4352]{1,0:T(8,128)}) %reduce-scatter.26.cloned.1.call-update) | async-done | bytes 2367504 | tf_op jit(solution)/shard_map/reduce_scatter | solution.py:92
  1386.6 7.3 fusion.49
  1394.1 7.2 multiply_reduce_fusion.1
  1402.7 28.0 %all-reduce.2 = f32[1088,12]{0,1:T(8,128)} all-reduce(f32[1088,12]{0,1:T(8,128)} %concatenate.8), channel_id=12, replica_groups=mesh['dp'=4,'ctx'=8] {'ctx'}, use_global_device_ids=true, to_apply=%region_34.35.clone | all-reduce | flops 13056 | bytes 104448
  1432.1 17.5 %all-reduce.3 = f32[136,12]{0,1:T(8,128)} all-reduce(f32[136,12]{0,1:T(8,128)} %constant_dynamic-slice_fusion.2), channel_id=13, replica_groups=mesh['dp'=4,'ctx'=8] {'dp'}, use_global_device_ids=true, to_apply=%region_35.36.clone | all-reduce | flops 1632 | bytes 13056
  1457.2 11.3 all-reduce.6.cloned.1.call-done
  1479.5 37.7 %reduce-scatter.30.cloned.1.call-done = f32[816,136]{1,0:T(8,128)} async-done(((f32[3264,136]{1,0:T(8,128)}), f32[816,136]{1,0:T(8,128)}) %reduce-scatter.30.cloned.1.call-update) | async-done | bytes 443920
  1521.3 53.7 %reduce-scatter.34.cloned.1.call-done = f32[1088,136]{1,0:T(8,128)} async-done(((f32[4352,136]{1,0:T(8,128)}), f32[1088,136]{1,0:T(8,128)}) %reduce-scatter.34.cloned.1.call-update) | async-done | bytes 591888
  (477 shorter events, 324.5 us)
Async XLA Ops:
  7.2 33.7 %all-gather.13.cloned.1.call-start = ((), (), s32[]{:S(2)}) async-start(), calls=%async_computation.9 | async-start | bytes 2193408 | tf_op jit(solution)/shard_map/all_gather | solution.py:73
  9.0 116.0 %all-gather.15.cloned.1.call-start = ((), (), s32[]{:S(2)}) async-start(), calls=%async_computation.10 | async-start | bytes 9400320 | tf_op jit(solution)/shard_map/all_gather | solution.py:80
  44.9 121.1 %all-gather.23.cloned.1.call-start = ((), (), s32[]{:S(2)}) async-start(), calls=%async_computation.14 | async-start | bytes 2820096 | tf_op jit(solution)/shard_map/all_gather | solution.py:75
  45.7 156.2 %all-gather.29.cloned.1.call-start = ((), (), s32[]{:S(2)}) async-start(), calls=%async_computation.22 | async-start | bytes 3133440 | tf_op jit(solution)/shard_map/all_gather | solution.py:76
  46.9 187.8 %all-gather.17.cloned.1.call-start = ((), (), s32[]{:S(2)}) async-start(), calls=%async_computation.11 | async-start | bytes 2506752 | tf_op jit(solution)/shard_map/all_gather | solution.py:107
  69.4 61.0 %copy-start.32 = (f32[1088]{0:T(1024)}, f32[1088]{0:T(1024)S(1)}, u32[]{:S(2)}) copy-start(f32[1088]{0:T(1024)S(1)} %get-tuple-element.323) | copy-start | bytes 13060
  69.4 61.0 %copy-start.34 = (f32[1088]{0:T(1024)}, f32[1088]{0:T(1024)S(1)}, u32[]{:S(2)}) copy-start(f32[1088]{0:T(1024)S(1)} %get-tuple-element.322) | copy-start | bytes 13060
  69.5 61.0 %copy-start.47 = (f32[128]{0:T(128)}, f32[128]{0:T(128)S(1)}, u32[]{:S(2)}) copy-start(f32[128]{0:T(128)S(1)} %broadcast_multiply_fusion.6) | copy-start | bytes 1540
  69.6 60.8 %copy-start.51 = (f32[128]{0:T(128)}, f32[128]{0:T(128)S(1)}, u32[]{:S(2)}) copy-start(f32[128]{0:T(128)S(1)} %add_rsqrt_fusion.1) | copy-start | bytes 1540
  131.2 136.1 %all-gather.19.cloned.1.call-start = ((), (), s32[]{:S(2)}) async-start(), calls=%async_computation.12 | async-start | bytes 2506752 | tf_op jit(solution)/shard_map/all_gather | solution.py:108
  132.5 209.8 %all-gather.21.cloned.1.call-start = ((), (), s32[]{:S(2)}) async-start(), calls=%async_computation.13 | async-start | bytes 3133440 | tf_op jit(solution)/shard_map/all_gather | solution.py:81
  155.0 255.4 %all-gather.25.cloned.1.call-start = ((), (), s32[]{:S(2)}) async-start(), calls=%async_computation.15 | async-start | bytes 12533760 | tf_op jit(solution)/shard_map/all_gather | solution.py:82
  171.2 337.6 %all-gather.27.cloned.1.call-start = ((), (), s32[]{:S(2)}) async-start(), calls=%async_computation.16 | async-start | bytes 11837440 | tf_op jit(solution)/shard_map/all_gather | solution.py:83
  207.4 502.5 %reduce-scatter.20.cloned.1.call-start = ((), (), s32[]{:S(2)}) async-start(), calls=%async_computation.17 | async-start | bytes 5013504 | tf_op jit(solution)/shard_map/reduce_scatter | solution.py:252
  272.6 70.4 %copy-start.37 = (f32[1088]{0:T(1024)S(1)}, f32[1088]{0:T(1024)}, u32[]{:S(2)}) copy-start(f32[1088]{0:T(1024)} %get-tuple-element.319) | copy-start | bytes 13060
  345.6 64.8 %copy-start.38 = (f32[128]{0:T(128)}, f32[128]{0:T(128)S(1)}, u32[]{:S(2)}) copy-start(f32[128]{0:T(128)S(1)} %broadcast_multiply_fusion.5) | copy-start | bytes 1540
  417.6 98.6 %copy-start.3 = (f32[128,4352]{1,0:T(8,128)}, f32[128,4352]{1,0:T(8,128)S(1)}, u32[]{:S(2)}) copy-start(f32[128,4352]{1,0:T(8,128)S(1)} %convolution_add_fusion) | copy-start | bytes 6684676
  522.2 135.9 %copy-start.5 = (f32[128,1088]{0,1:T(8,128)}, f32[128,1088]{0,1:T(8,128)S(1)}, u32[]{:S(2)}) copy-start(f32[128,1088]{0,1:T(8,128)S(1)} %get-tuple-element.382) | copy-start | bytes 1671172
  657.3 105.8 %reduce-scatter.22.cloned.1.call-start = ((), (), s32[]{:S(2)}) async-start(), calls=%async_computation.18 | async-start | bytes 5013504 | tf_op jit(solution)/shard_map/reduce_scatter | solution.py:253
  658.0 163.6 %reduce-scatter.36.cloned.1.call-start = ((), (), s32[]{:S(2)}) async-start(), calls=%async_computation.27 | async-start | bytes 5640192
  661.1 360.4 %reduce-scatter.28.cloned.1.call-start = ((), (), s32[]{:S(2)}) async-start(), calls=%async_computation.21 | async-start | bytes 22560768 | tf_op jit(solution)/shard_map/reduce_scatter | solution.py:93
  672.4 93.5 %copy-start.48 = (f32[128]{0:T(128)S(1)}, f32[128]{0:T(128)}, u32[]{:S(2)}) copy-start(f32[128]{0:T(128)} %copy-done.47) | copy-start | bytes 1540
  672.4 496.9 %reduce-scatter.24.cloned.1.call-start = ((), (), s32[]{:S(2)}) async-start(), calls=%async_computation.19 | async-start | bytes 16293888 | tf_op jit(solution)/shard_map/reduce_scatter | solution.py:90
  774.3 584.6 %reduce-scatter.26.cloned.1.call-start = ((), (), s32[]{:S(2)}) async-start(), calls=%async_computation.20 | async-start | bytes 21307392 | tf_op jit(solution)/shard_map/reduce_scatter | solution.py:92
  784.5 669.5 %reduce-scatter.32.cloned.1.call-start = ((), (), s32[]{:S(2)}) async-start(), calls=%async_computation.24 | async-start | bytes 1392640
  824.1 644.4 %all-reduce.6.cloned.1.call-start = ((), (), s32[]{:S(2)}) async-start(), calls=%async_computation.26 | async-start | bytes 5013504
  1021.5 495.6 %reduce-scatter.30.cloned.1.call-start = ((), (), s32[]{:S(2)}) async-start(), calls=%async_computation.23 | async-start | bytes 4177920
  1172.7 402.3 %reduce-scatter.34.cloned.1.call-start = ((), (), s32[]{:S(2)}) async-start(), calls=%async_computation.25 | async-start | bytes 5570560
  1394.0 58.2 %copy-start.6 = (f32[128,1088]{0,1:T(8,128)S(1)}, f32[128,1088]{0,1:T(8,128)}, u32[]{:S(2)}) copy-start(f32[128,1088]{0,1:T(8,128)} %copy-done.5) | copy-start | bytes 1671172
  1402.7 65.9 %copy-start.9 = (f32[544,272]{1,0:T(8,128)S(1)}, f32[544,272]{1,0:T(8,128)}, u32[]{:S(2)}) copy-start(f32[544,272]{1,0:T(8,128)} %copy.103) | copy-start | bytes 1775620
  1402.7 65.9 %copy-start.10 = (f32[544,272]{1,0:T(8,128)S(1)}, f32[544,272]{1,0:T(8,128)}, u32[]{:S(2)}) copy-start(f32[544,272]{1,0:T(8,128)} %copy.100) | copy-start | bytes 1775620
  1518.6 58.0 %copy-start.30 = (f32[136,1088]{1,0:T(8,128)S(1)}, f32[136,1088]{1,0:T(8,128)}, u32[]{:S(2)}) copy-start(f32[136,1088]{1,0:T(8,128)} %param.32) | copy-start | bytes 1775620
  (44 other events, 428.7 us)
Sparse Core Ops, SparseCore 0:
  10.2 30.6 all-gather.12
  45.0 79.9 all-gather.14
  127.2 38.7 all-gather.22
  168.1 33.8 all-gather.28
  203.9 30.6 all-gather.16
  236.7 30.5 all-gather.18
  269.7 37.5 all-gather.20
  309.2 101.1 all-gather.24
  412.2 96.4 all-gather.26
  657.4 52.3 reduce-scatter.19
  712.2 50.8 reduce-scatter.21
  765.3 56.3 reduce-scatter.35
  824.0 197.4 reduce-scatter.27
  1023.7 145.5 reduce-scatter.23
  1171.4 187.4 reduce-scatter.25
  1361.8 26.8 reduce-scatter.31
  1391.7 76.8 all-reduce.5
  1471.4 45.6 reduce-scatter.29
  1520.2 54.7 reduce-scatter.33
where the time goes:
time: 1600 us; the launch traced here: 1590 us
  waiting for transfers between devices  1090 us (68%)
  matrix products  234 us (15%)
  local copies, waits for them, and re-layouts  113 us (7%)
  blocking collectives  88.3 us (6%)
  other arithmetic  38.1 us (2%)
  between operations  17 us (1%)
    reduce_scatter x1, waiting for transfers between devices, reduce_grads(): lax.psum_scatter(fourth_part, 'ctx', scatter_dimension=0, tiled=True)  197 us
    reduce_scatter x1, waiting for transfers between devices, reduce_grads(): lax.psum_scatter(third_part, 'ctx', scatter_dimension=0, tiled=True)  186 us
    reduce_scatter x1, waiting for transfers between devices, reduce_grads(): lax.psum_scatter(first_part, 'ctx', scatter_dimension=0, tiled=True)  148 us
    unnamed x24, waiting for transfers between devices  141 us
    all_gather x1, waiting for transfers between devices, gather_params(): lax.all_gather(piece_four, 'dp', axis=1, tiled=True)  91.1 us
    all_gather x1, waiting for transfers between devices, gather_params(): lax.all_gather(piece_three, 'dp', axis=1, tiled=True)  64.1 us
    all_gather x1, waiting for transfers between devices, gather_params(): lax.all_gather(piece_one, 'dp', axis=1, tiled=True)  55.4 us
    reduce_scatter x1, waiting for transfers between devices, local(): lax.psum_scatter(join_heads(dvalue_heads), 'ctx', scatter_dimension=0, ti...  51.4 us
  transfers between devices with their start and end apart: 19, of which 17 were waited for; matrix products, arithmetic and copies ran while one was open for 14% of the time, Pallas kernels for 0%

commit v1 on v0

v1 whole, which is shorter than its diff:
```python
import jax
import jax.numpy as jnp
from jax import lax
from jax.experimental import pallas as pl
from jax.experimental.pallas import tpu as pltpu
from jax.sharding import PartitionSpec as P

D = 1088
H = 17
HD = 64
BLK = 64


norm_eps = 1e-05
beta_first = 0.9
beta_second = 0.95
learn_rate = 0.01
decay_rate = 0.1
adam_eps = 1e-08
adam_steps = 4
gelu_coef = 0.7978845608028654
masked_score = -1e30


def layer_norm(values):
    center = jnp.mean(values, axis=-1, keepdims=True)
    shifted = values - center
    inverse = lax.rsqrt(jnp.mean(shifted * shifted, axis=-1, keepdims=True) + norm_eps)
    return (shifted * inverse, inverse)


def norm_back(incoming, normed, inverse, gain_vec):
    scaled = incoming * gain_vec
    return inverse * (
        scaled
        - jnp.mean(scaled, axis=-1, keepdims=True)
        - normed * jnp.mean(scaled * normed, axis=-1, keepdims=True)
    )


def gelu_value(values):
    inside = gelu_coef * (values + 0.044715 * values * values * values)
    return 0.5 * values * (1.0 + jnp.tanh(inside))


def gelu_slope(values):
    inside = gelu_coef * (values + 0.044715 * values * values * values)
    tangent = jnp.tanh(inside)
    return 0.5 * (1.0 + tangent) + 0.5 * values * (1.0 - tangent * tangent) * gelu_coef * (
        1.0 + 3.0 * 0.044715 * values * values
    )


def adam_update(weight, gradient, moment, square, decayed):
    moment_new = beta_first * moment + (1.0 - beta_first) * gradient
    square_new = beta_second * square + (1.0 - beta_second) * gradient * gradient
    first_fix = 1.0 - beta_first**adam_steps
    second_fix = 1.0 - beta_second**adam_steps
    direction = moment_new / first_fix / (jnp.sqrt(square_new / second_fix) + adam_eps)
    if decayed:
        direction = direction + decay_rate * weight
    return (weight - learn_rate * direction, moment_new, square_new)


def dot_on(left, right, left_dim, right_dim):
    return lax.dot_general(
        left, right, (((left_dim,), (right_dim,)), ((), ())), preferred_element_type=jnp.float32
    )


def head_probs(query_t, key_t, allowed):
    scores = dot_on(query_t, key_t, 0, 0) * HD ** (-0.5)
    scores = jnp.where(allowed, scores, masked_score)
    row_max = jnp.max(scores, axis=1, keepdims=True)
    weights = jnp.exp(scores - row_max)
    return weights / jnp.sum(weights, axis=1, keepdims=True)


def forward_kernel(query_pos, key_pos, query_ref, key_ref, value_ref, out_ref):
    allowed = query_pos[...] >= key_pos[...]
    probs = head_probs(query_ref[...], key_ref[...], allowed).astype(jnp.bfloat16)
    out_ref[...] = dot_on(value_ref[...], probs, 1, 1).astype(jnp.bfloat16)


def backward_kernel(
    query_pos, key_pos, query_ref, key_ref, value_ref, out_ref, dout_ref, dquery, dkey, dvalue
):
    allowed = query_pos[...] >= key_pos[...]
    query_t = query_ref[...]
    key_t = key_ref[...]
    dout_t = dout_ref[...]
    probs = head_probs(query_t, key_t, allowed)
    dprobs = dot_on(dout_t, value_ref[...], 0, 0)
    products = dout_t.astype(jnp.float32) * out_ref[...].astype(jnp.float32)
    delta = jnp.sum(products.T, axis=1, keepdims=True)
    dscores = (probs * (dprobs - delta) * HD ** (-0.5)).astype(jnp.bfloat16)
    dquery[...] = dot_on(key_t, dscores, 1, 1).astype(jnp.bfloat16)
    dkey[...] = dot_on(query_t, dscores, 1, 0).astype(jnp.bfloat16)
    dvalue[...] = dot_on(dout_t, probs.astype(jnp.bfloat16), 1, 0).astype(jnp.bfloat16)


def attention(kernel, query_pos, key_pos, features, out_rows):
    queries, keys = query_pos.shape[0], key_pos.shape[1]
    whole = lambda array: pl.BlockSpec(array.shape, lambda h: (0, 0))
    block = lambda width: pl.BlockSpec((HD, width), lambda h: (h, 0))
    shapes = [jax.ShapeDtypeStruct((H * HD, width), jnp.bfloat16) for width in out_rows]
    flops = 2 * H * HD * queries * keys * (2 if len(out_rows) == 1 else 5)
    return pl.pallas_call(
        kernel,
        grid=(H,),
        in_specs=[whole(query_pos), whole(key_pos)] + [block(x.shape[1]) for x in features],
        out_specs=[block(width) for width in out_rows],
        out_shape=shapes,
        cost_estimate=pl.CostEstimate(
            flops=flops, bytes_accessed=8 * H * HD * keys, transcendentals=H * queries * keys
        ),
    )(query_pos, key_pos, *features)


def exchange(blocks):
    return lax.all_to_all(blocks, "ctx", split_axis=0, concat_axis=0, tiled=True)


def scatter_rows(partial):
    return lax.psum_scatter(
        partial.astype(jnp.bfloat16), "ctx", scatter_dimension=0, tiled=True
    ).astype(jnp.float32)


def gather_rows(rows):
    return lax.all_gather(rows, "ctx", axis=0, tiled=True)


def local(
    inputs,
    out_grad,
    pair_blocks,
    triple_weight,
    merge_weight,
    expand_weight,
    shrink_weight,
    vector_params,
    triple_moment,
    merge_moment,
    expand_moment,
    shrink_moment,
    vector_moment,
    triple_square,
    merge_square,
    expand_square,
    shrink_square,
    vector_square,
):
    bf16 = jnp.bfloat16
    n = lax.axis_size("ctx")
    m = lax.axis_size("dp")
    here = lax.axis_index("ctx")
    rows = inputs.shape[1]
    total = rows * n
    feat = D // n
    hidden_width = m * expand_weight.shape[1]
    wide = hidden_width // n
    stream = inputs[0]
    cotangent = out_grad[0]
    offsets = jnp.arange(BLK, dtype=jnp.int32)
    positions = (pair_blocks.reshape(-1)[:, None] * BLK + offsets[None, :]).reshape(-1)
    query_pos = lax.dynamic_slice_in_dim(positions, here * rows, rows)[:, None]
    key_pos = positions[None, :]

    packed = jnp.concatenate(
        [
            triple_weight.astype(bf16),
            merge_weight.astype(bf16),
            expand_weight.astype(bf16),
            vector_params.astype(bf16),
        ],
        axis=1,
    )
    tw, mw, ew = triple_weight.shape[1], merge_weight.shape[1], expand_weight.shape[1]
    columns = lax.all_gather(packed, "dp", axis=0)

    def take(start, width):
        return columns[:, :, start : start + width].transpose(1, 0, 2).reshape(feat, m * width)

    triple_rows = take(0, tw)
    merge_rows = take(tw, mw)
    expand_rows = take(tw + mw, ew)
    vector_rows = take(tw + mw + ew, vector_params.shape[1])
    normed_one, inverse_one = layer_norm(stream)
    normed_full = gather_rows(normed_one.astype(bf16))
    send = jnp.concatenate(
        [
            triple_rows.reshape(feat, 3, n, feat).transpose(2, 0, 1, 3).reshape(n, feat, 3 * feat),
            expand_rows.reshape(feat, n, wide).transpose(1, 0, 2),
        ],
        axis=2,
    )
    got = exchange(send).reshape(D, 3 * feat + wide)
    w_triple = got[:, : 3 * feat]
    w_expand = got[:, 3 * feat :]
    merged = gather_rows(jnp.concatenate([merge_rows, vector_rows], axis=1))
    w_merge = merged[:, :D]
    vectors = merged[:, D:].astype(jnp.float32)
    gain_one = vectors[:, 0]
    shift_one = vectors[:, 1]
    query_bias = lax.dynamic_slice_in_dim(vectors[:, 2], here * feat, feat)
    value_bias = lax.dynamic_slice_in_dim(vectors[:, 3], here * feat, feat)
    merge_bias = vectors[:, 4]
    gain_two = vectors[:, 5]
    shift_two = vectors[:, 6]
    shrink_bias = vectors[:, 7]
    expand_bias = lax.dynamic_slice_in_dim(vectors[:, 8:].T.reshape(-1), here * wide, wide)

    act_one = (normed_full.astype(jnp.float32) * gain_one + shift_one).astype(bf16)
    bias = jnp.concatenate([query_bias, jnp.zeros_like(query_bias), value_bias])
    triple_t = (dot_on(w_triple, act_one, 0, 1) + bias[:, None]).astype(bf16)
    query_t = exchange(triple_t[:feat].reshape(feat, n, rows).transpose(1, 0, 2)).reshape(D, rows)
    both = lax.all_gather(triple_t[feat:].reshape(2, feat, total), "ctx", axis=0)
    key_t = both[:, 0].reshape(D, total)
    value_t = both[:, 1].reshape(D, total)
    (attended_t,) = attention(
        forward_kernel, query_pos, key_pos, (query_t, key_t, value_t), (rows,)
    )
    cot_full = gather_rows(cotangent.astype(bf16))
    w_shrink = (
        lax.all_gather(shrink_weight.astype(bf16), "dp", axis=0).transpose(1, 0, 2).reshape(wide, D)
    )
    middle = stream + dot_on(attended_t, w_merge, 0, 0) + merge_bias
    normed_two, inverse_two = layer_norm(middle)
    act_two = gather_rows((normed_two * gain_two + shift_two).astype(bf16))
    pre_act = dot_on(act_two, w_expand, 1, 0) + expand_bias
    hidden_b = gelu_value(pre_act).astype(bf16)
    dpre = dot_on(cot_full, w_shrink, 1, 1) * gelu_slope(pre_act)
    dpre_b = dpre.astype(bf16)
    expand_bias_grad = jnp.sum(dpre, axis=0)
    dact_two = scatter_rows(dot_on(dpre_b, w_expand, 1, 1))
    block_out = middle + scatter_rows(dot_on(hidden_b, w_shrink, 1, 0)) + shrink_bias
    shrink_part = dot_on(hidden_b, cot_full, 0, 0).astype(bf16)
    expand_part = dot_on(act_two, dpre_b, 0, 0).astype(bf16)
    shrink_grad = lax.psum_scatter(
        shrink_part.reshape(wide, m, D // m).transpose(1, 0, 2), "dp", scatter_dimension=0
    ).astype(jnp.float32)
    shrink_bias_grad = jnp.sum(cotangent, axis=0)
    gain_two_grad = jnp.sum(dact_two * normed_two, axis=0)
    shift_two_grad = jnp.sum(dact_two, axis=0)
    dmiddle = cotangent + norm_back(dact_two, normed_two, inverse_two, gain_two)
    dmiddle_b = dmiddle.astype(bf16)
    merge_part = lax.psum_scatter(
        dot_on(attended_t, dmiddle_b, 1, 0).astype(bf16), "ctx", scatter_dimension=0, tiled=True
    )
    merge_bias_grad = jnp.sum(dmiddle, axis=0)
    dattended_t = dot_on(w_merge, dmiddle_b, 1, 1).astype(bf16)
    dquery_t, dkey_t, dvalue_t = attention(
        backward_kernel,
        query_pos,
        key_pos,
        (query_t, key_t, value_t, attended_t, dattended_t),
        (rows, total, total),
    )
    dquery_c = exchange(dquery_t.reshape(n, feat, rows)).transpose(1, 0, 2).reshape(feat, total)
    dkey_c = lax.psum_scatter(dkey_t, "ctx", scatter_dimension=0, tiled=True)
    dvalue_c = lax.psum_scatter(dvalue_t, "ctx", scatter_dimension=0, tiled=True)
    dtriple_t = jnp.concatenate([dquery_c, dkey_c, dvalue_c], axis=0)
    query_bias_grad = jnp.sum(dquery_c.astype(jnp.float32), axis=1)
    value_bias_grad = jnp.sum(dvalue_c.astype(jnp.float32), axis=1)
    dact_one = scatter_rows(dot_on(dtriple_t, w_triple, 0, 1))
    triple_part = dot_on(act_one, dtriple_t, 0, 1).astype(bf16)
    gain_one_grad = jnp.sum(dact_one * normed_one, axis=0)
    shift_one_grad = jnp.sum(dact_one, axis=0)
    input_rows = dmiddle + norm_back(dact_one, normed_one, inverse_one, gain_one)

    def place(piece, size):
        return lax.dynamic_update_slice_in_dim(
            jnp.zeros((size,), jnp.float32), piece, here * piece.shape[0], 0
        )

    vector_local = jnp.concatenate(
        [
            jnp.stack(
                [
                    gain_one_grad,
                    shift_one_grad,
                    place(query_bias_grad, D),
                    place(value_bias_grad, D),
                    merge_bias_grad,
                    gain_two_grad,
                    shift_two_grad,
                    shrink_bias_grad,
                ],
                axis=1,
            ),
            place(expand_bias_grad, hidden_width).reshape(-1, D).T,
        ],
        axis=1,
    )
    vector_part = lax.psum_scatter(vector_local, "ctx", scatter_dimension=0, tiled=True)

    def by_dp(rows_part):
        return rows_part.reshape(feat, m, -1).transpose(1, 0, 2)

    expand_rows_part = exchange(expand_part.reshape(n, feat, wide)).transpose(1, 0, 2)
    expand_grad = lax.psum_scatter(by_dp(expand_rows_part), "dp", scatter_dimension=0).astype(
        jnp.float32
    )
    triple_rows_part = (
        exchange(triple_part.reshape(n, feat, 3 * feat))
        .reshape(n, feat, 3, feat)
        .transpose(1, 2, 0, 3)
    )
    last = lax.psum_scatter(
        jnp.concatenate(
            [by_dp(triple_rows_part), by_dp(merge_part), by_dp(vector_part).astype(bf16)], axis=2
        ),
        "dp",
        scatter_dimension=0,
    ).astype(jnp.float32)
    triple_grad = last[:, :tw]
    merge_grad = last[:, tw : tw + mw]
    vector_grad = last[:, tw + mw :]
    triple_new, triple_moment_new, triple_square_new = adam_update(
        triple_weight, triple_grad, triple_moment, triple_square, True
    )
    merge_new, merge_moment_new, merge_square_new = adam_update(
        merge_weight, merge_grad, merge_moment, merge_square, True
    )
    expand_new, expand_moment_new, expand_square_new = adam_update(
        expand_weight, expand_grad, expand_moment, expand_square, True
    )
    shrink_new, shrink_moment_new, shrink_square_new = adam_update(
        shrink_weight, shrink_grad, shrink_moment, shrink_square, True
    )
    vector_new, vector_moment_new, vector_square_new = adam_update(
        vector_params, vector_grad, vector_moment, vector_square, False
    )
    return (
        block_out[None],
        input_rows[None],
        triple_grad,
        merge_grad,
        expand_grad,
        shrink_grad,
        vector_grad,
        triple_new,
        merge_new,
        expand_new,
        shrink_new,
        vector_new,
        triple_moment_new,
        merge_moment_new,
        expand_moment_new,
        shrink_moment_new,
        vector_moment_new,
        triple_square_new,
        merge_square_new,
        expand_square_new,
        shrink_square_new,
        vector_square_new,
    )


def solution(mesh):
    in_specs = (
        P("dp", "ctx", None),
        P("dp", "ctx", None),
        P(),
        P("ctx", "dp"),
        P("ctx", "dp"),
        P("ctx", "dp"),
        P("ctx", "dp"),
        P("ctx", "dp"),
        P("ctx", "dp"),
        P("ctx", "dp"),
        P("ctx", "dp"),
        P("ctx", "dp"),
        P("ctx", "dp"),
        P("ctx", "dp"),
        P("ctx", "dp"),
        P("ctx", "dp"),
        P("ctx", "dp"),
        P("ctx", "dp"),
    )
    out_specs = (
        P("dp", "ctx", None),
        P("dp", "ctx", None),
        P("ctx", "dp"),
        P("ctx", "dp"),
        P("ctx", "dp"),
        P("ctx", "dp"),
        P("ctx", "dp"),
        P("ctx", "dp"),
        P("ctx", "dp"),
        P("ctx", "dp"),
        P("ctx", "dp"),
        P("ctx", "dp"),
        P("ctx", "dp"),
        P("ctx", "dp"),
        P("ctx", "dp"),
        P("ctx", "dp"),
        P("ctx", "dp"),
        P("ctx", "dp"),
        P("ctx", "dp"),
        P("ctx", "dp"),
        P("ctx", "dp"),
        P("ctx", "dp"),
    )
    return jax.shard_map(local, mesh=mesh, in_specs=in_specs, out_specs=out_specs, check_vma=False)
```

time: 1600 us -> 794 us (0.50)
  waiting for transfers between devices: 1090 us -> 445 us
  matrix products: 234 us -> 48.5 us
  Pallas kernels: 0 us -> 34.4 us
    reduce_scatter x5 -> x2, waiting for transfers between devices: 618 us -> 54.3 us  [the longest x1 37 us: local(): lax.psum_scatter(dvalue_t, 'ctx', scatter_dimension=0, tiled=True)]
    dot_general x131 -> x12, matrix products: 234 us -> 48.5 us  [dot_on(): lax.dot_general(left, right, (((left_dim,), (right_dim,)), ((), ())), pre...]
    all_gather x9 -> x7, waiting for transfers between devices: 335 us -> 243 us  [the longest x4 126 us: gather_rows(): return lax.all_gather(rows, 'ctx', axis=0, tiled=True)]
    all_to_all x0 -> x2, blocking collectives: none -> 65 us  [exchange(): lax.all_to_all(blocks, 'ctx', split_axis=0, concat_axis=0, tiled=True)]
    all_gather x3 -> x0, blocking collectives: 42.8 us -> none  [the longest x1 21.3 us: gather_params(): lax.all_gather(second_part, 'ctx', axis=0, tiled=True)]
    all_to_all x0 -> x3, waiting for transfers between devices: none -> 36.3 us  [exchange(): lax.all_to_all(blocks, 'ctx', split_axis=0, concat_axis=0, tiled=True)]
    pallas_call x0 -> x2, Pallas kernels: none -> 34.4 us  [attention(): pl.pallas_call(kernel, grid=(H,), in_specs=[whole(query_pos), whole(key_p...]
    unnamed x24 -> x23, waiting for transfers between devices: 141 us -> 111 us
  transfers between devices with their start and end apart: 19 -> 19, of which waited for: 17 -> 15; matrix products, arithmetic and copies ran while one was open for 14% -> 14% of each run, Pallas kernels for 0% -> 0%
where the time goes in v1:
time: 794 us; the launch traced here: 783 us
  waiting for transfers between devices  445 us (56%)
  local copies, waits for them, and re-layouts  107 us (13%)
  blocking collectives  93.1 us (12%)
  matrix products  48.5 us (6%)
  Pallas kernels  34.4 us (4%)
  other arithmetic  26.7 us (3%)
  between operations  15.5 us (2%)
  starting transfers between devices  12.9 us (2%)
    all_gather x4, waiting for transfers between devices, gather_rows(): return lax.all_gather(rows, 'ctx', axis=0, tiled=True)  126 us
    unnamed x23, waiting for transfers between devices  111 us
    all_to_all x2, blocking collectives, exchange(): lax.all_to_all(blocks, 'ctx', split_axis=0, concat_axis=0, tiled=True)  65 us
    dot_general x12, matrix products, dot_on(): lax.dot_general(left, right, (((left_dim,), (right_dim,)), ((), ())), pre...  48.5 us
    all_gather x1, waiting for transfers between devices, local(): lax.all_gather(triple_t[feat:].reshape(2, feat, total), 'ctx', axis=0)  46.7 us
    unnamed x93, local copies, waits for them, and re-layouts  44.4 us
    all_gather x1, waiting for transfers between devices, local(): columns = lax.all_gather(packed, 'dp', axis=0)  41.4 us
    reduce_scatter x1, waiting for transfers between devices, local(): lax.psum_scatter(dvalue_t, 'ctx', scatter_dimension=0, tiled=True)  37 us
  transfers between devices with their start and end apart: 19, of which 15 were waited for; matrix products, arithmetic and copies ran while one was open for 14% of the time, Pallas kernels for 0%

profile of v1, /device:TPU:0, one launch (start us, length us, event | category | flops | bytes accessed | tf_op | source)
XLA Modules:
  0.0 782.9 jit_solution(6894993608539550052)
XLA Ops:
  12.9 41.4 %all-gather.21.cloned.1.call-done = bf16[544,2179]{1,0:T(8,128)(2,1)} async-done(((bf16[136,2179]{1,0:T(8,128)(2,1)}), bf16[544,2179]{1,0:T(8,128)(2,1)}) %all-gather.21.cloned.1.call-update) | async-done | bytes 2370768 | tf_op jit(solution)/shard_map/all_gather | solution.py:180
  78.2 4.6 all-to-all-start
  82.8 14.6 %all-gather.13.cloned.1.call-done = bf16[1088,1100]{1,0:T(8,128)(2,1)} async-done(((bf16[136,1100]{1,0:T(8,128)(2,1)}), bf16[1088,1100]{1,0:T(8,128)(2,1)}) %all-gather.13.cloned.1.call-update) | async-done | bytes 2393616 | tf_op jit(solution)/shard_map/all_gather | solution.py:131
  100.7 55.9 %all-gather.11.cloned.1.call-done = bf16[1024,1088]{0,1:T(8,128)(2,1)} async-done(((bf16[128,1088]{0,1:T(8,128)(2,1)}), bf16[1024,1088]{0,1:T(8,128)(2,1)}) %all-gather.11.cloned.1.call-update) | async-done | bytes 2228240 | tf_op jit(solution)/shard_map/all_gather | solution.py:131
  157.2 3.9 add_convert_fusion.1
  169.5 46.7 %all-gather.15.cloned.1.call-done = bf16[8,2,136,1024]{3,2,0,1:T(8,128)(2,1)} async-done(((bf16[1,2,136,1024]{3,2,0,1:T(8,128)(2,1)}), bf16[8,2,136,1024]{3,2,0,1:T(8,128)(2,1)}) %all-gather.15.cloned.1.call-update) | async-done | bytes 4456464 | tf_op jit(solution)/shard_map/all_gather | solution.py:218
  216.1 4.9 fusion.49
  221.8 16.2 %shard_map.345.out_ref = bf16[1088,128]{1,0:T(8,128)(2,1)} custom-call(s32[128,1]{1,0:T(8,128)} %copy.197.query_pos, s32[1,1024]{1,0:T(1,128)} %add.235.key_pos, bf16[1088,128]{1,0:T(8,128)(2,1)} %bitcast.139, bf16[1088,1024]{1,0:T(8,128)(2,1)} %bitcast.122, bf16[1088,1024]{1,0:T(8,128)(2,1)} %bitcast.120), custom_call_target="tpu_custom_call" | custom-call | flops 570425344 | bytes 8912896 | tf_op jit(solution)/shard_map/pallas_call | solution.py:108
  243.8 29.1 %all-gather.17.cloned.1.call-done = bf16[1024,1088]{0,1:T(8,128)(2,1)} async-done(((bf16[128,1088]{0,1:T(8,128)(2,1)}), bf16[1024,1088]{0,1:T(8,128)(2,1)}) %all-gather.17.cloned.1.call-update) | async-done | bytes 2228240 | tf_op jit(solution)/shard_map/all_gather | solution.py:131
  272.9 5.8 fusion.10
  278.6 26.9 %all-gather.19.cloned.1.call-done = bf16[1024,1088]{0,1:T(8,128)(2,1)} async-done(((bf16[128,1088]{0,1:T(8,128)(2,1)}), bf16[1024,1088]{0,1:T(8,128)(2,1)}) %all-gather.19.cloned.1.call-update) | async-done | bytes 2228240 | tf_op jit(solution)/shard_map/all_gather | solution.py:131
  305.5 5.5 convolution_convert_fusion.4
  313.7 30.0 %reduce-scatter.41.cloned.1.call-done = bf16[1,544,272]{1,2,0:T(8,128)(2,1)} async-done(((bf16[4,544,272]{1,2,0:T(8,128)(2,1)}), bf16[1,544,272]{1,2,0:T(8,128)(2,1)}) %reduce-scatter.41.cloned.1.call-update) | async-done | bytes 295952
  347.3 29.1 %all-gather.23.cloned.1.call-done = bf16[4,544,272]{1,2,0:T(8,128)(2,1)} async-done(((bf16[1,544,272]{1,2,0:T(8,128)(2,1)}), bf16[4,544,272]{1,2,0:T(8,128)(2,1)}) %all-gather.23.cloned.1.call-update) | async-done | bytes 1183760 | tf_op jit(solution)/shard_map/all_gather | solution.py:226
  376.3 5.8 fusion.52
  386.5 4.2 copy.229
  390.8 5.6 convolution_convert_fusion.2
  396.4 4.2 copy.227
  400.7 27.3 %reduce-scatter.31.cloned.1.call-done = bf16[128,1088]{1,0:T(8,128)(2,1)} async-done(((bf16[1024,1088]{1,0:T(8,128)(2,1)}), bf16[128,1088]{1,0:T(8,128)(2,1)}) %reduce-scatter.31.cloned.1.call-update) | async-done | bytes 278544
  429.6 36.5 %reduce-scatter.29.cloned.1.call-done = bf16[128,1088]{1,0:T(8,128)(2,1)} async-done(((bf16[1024,1088]{1,0:T(8,128)(2,1)}), bf16[128,1088]{1,0:T(8,128)(2,1)}) %reduce-scatter.29.cloned.1.call-update) | async-done | bytes 278544
  470.7 18.3 %shard_map.346 = (bf16[1088,128]{1,0:T(8,128)(2,1)}, bf16[1088,1024]{1,0:T(8,128)(2,1)}, bf16[1088,1024]{1,0:T(8,128)(2,1)}) custom-call(s32[128,1]{1,0:T(8,128)} %copy.197.query_pos, s32[1,1024]{1,0:T(1,128)} %add.235.key_pos, bf16[1088,128]{1,0:T(8,128)(2,1)} %bitcast.140, bf16[1088,1024]{1,0:T(8,128)(2,1)} %bitcast.123, bf16[1088,1024]{1,0:T(8,128)(2,1)} %bitcast.121, ...), custom_call_target="tpu_custom_call" | custom-call | flops 1426063360 | bytes 8912896 | tf_op jit(solution)/shard_map/pallas_call | solution.py:108
  492.3 17.5 %all_to_all.25 = bf16[8,136,128]{2,1,0:T(8,128)(2,1)S(1)} all-to-all(bf16[8,136,128]{2,1,0:T(8,128)(2,1)S(1)} %bitcast.149), channel_id=1, replica_groups=mesh['dp'=4,'ctx'=8] {'ctx'}, dimensions={0} | all-to-all | bytes 557056 | tf_op jit(solution)/shard_map/all_to_all | solution.py:121
  509.8 17.3 %reduce-scatter.25.cloned.1.call-done = bf16[136,1024]{1,0:T(8,128)(2,1)} async-done(((bf16[1088,1024]{1,0:T(8,128)(2,1)}), bf16[136,1024]{1,0:T(8,128)(2,1)}) %reduce-scatter.25.cloned.1.call-update) | async-done | bytes 278544 | tf_op jit(solution)/shard_map/reduce_scatter | solution.py:261
  528.0 37.0 %reduce-scatter.27.cloned.1.call-done = bf16[136,1024]{1,0:T(8,128)(2,1)} async-done(((bf16[1088,1024]{1,0:T(8,128)(2,1)}), bf16[136,1024]{1,0:T(8,128)(2,1)}) %reduce-scatter.27.cloned.1.call-update) | async-done | bytes 278544 | tf_op jit(solution)/shard_map/reduce_scatter | solution.py:262
  566.0 4.3 convolution_convert_fusion.3
  570.3 4.3 copy.231
  575.8 4.3 convolution_convert_fusion.5
  582.6 47.5 %all_to_all.26 = bf16[8,136,544]{2,1,0:T(8,128)(2,1)S(1)} all-to-all(bf16[8,136,544]{2,1,0:T(8,128)(2,1)S(1)} %bitcast.129), channel_id=1, replica_groups=mesh['dp'=4,'ctx'=8] {'ctx'}, dimensions={0} | all-to-all | bytes 2367488 | tf_op jit(solution)/shard_map/all_to_all | solution.py:121
  647.7 35.7 %all-to-all-done.3 = bf16[8,136,408]{2,1,0:T(8,128)(2,1)S(1)} async-done(((bf16[8,136,408]{2,1,0:T(8,128)(2,1)}), bf16[8,136,408]{2,1,0:T(8,128)(2,1)S(1)}, u32[]{:S(2)}, u32[]{:S(2)}) %all-to-all-start.3) | async-done | bytes 887840 | tf_op jit(solution)/shard_map/all_to_all | solution.py:121
  693.1 28.1 %all-reduce.1 = bf16[1088,12]{0,1:T(8,128)(2,1)S(1)} all-reduce(f32[1088,12]{0,1:T(8,128)S(1)} %concatenate.26), channel_id=10, replica_groups=mesh['dp'=4,'ctx'=8] {'ctx'}, use_global_device_ids=true, to_apply=%region_23.0.clone | all-reduce | flops 13056 | bytes 78336
  721.6 4.6 concatenate.27
  738.9 16.2 %reduce-scatter.37.cloned.1.call-done = bf16[1,136,1091]{2,1,0:T(8,128)(2,1)} async-done(((bf16[4,136,1091]{2,1,0:T(8,128)(2,1)}), bf16[1,136,1091]{2,1,0:T(8,128)(2,1)}) %reduce-scatter.37.cloned.1.call-update) | async-done | bytes 296768
  (229 shorter events, 134.3 us)
Async XLA Ops:
  7.2 47.1 %all-gather.21.cloned.1.call-start = ((), (), s32[]{:S(2)}) async-start(), calls=%async_computation.21 | async-start | bytes 3133440 | tf_op jit(solution)/shard_map/all_gather | solution.py:180
  12.9 47.1 %copy-start = (f32[1,128,1088]{1,2,0:T(8,128)S(1)}, f32[1,128,1088]{1,2,0:T(8,128)}, u32[]{:S(2)}) copy-start(f32[1,128,1088]{1,2,0:T(8,128)} %param.18) | copy-start | bytes 1671172
  12.9 84.5 %all-gather.13.cloned.1.call-start = ((), (), s32[]{:S(2)}) async-start(), calls=%async_computation.15 | async-start | bytes 2820096 | tf_op jit(solution)/shard_map/all_gather | solution.py:131
  59.9 96.7 %all-gather.11.cloned.1.call-start = ((), (), s32[]{:S(2)}) async-start(), calls=%async_computation.14 | async-start | bytes 2506752 | tf_op jit(solution)/shard_map/all_gather | solution.py:131
  78.2 79.0 %all-to-all-start = ((bf16[8,136,952]{2,1,0:T(8,128)(2,1)}), bf16[8,136,952]{2,1,0:T(8,128)(2,1)S(1)}, u32[]{:S(2)}, u32[]{:S(2)}) async-start(bf16[8,136,952]{2,1,0:T(8,128)(2,1)} %copy.191), calls=%async_computation | async-start | bytes 4456448 | tf_op jit(solution)/shard_map/all_to_all | solution.py:121
  82.8 133.4 %all-gather.15.cloned.1.call-start = ((), (), s32[]{:S(2)}) async-start(), calls=%async_computation.16 | async-start | bytes 5013504 | tf_op jit(solution)/shard_map/all_gather | solution.py:218
  165.0 56.1 %all-to-all-start.1 = ((bf16[8,136,128]{2,1,0:T(8,128)(2,1)}), bf16[8,136,128]{2,1,0:T(8,128)(2,1)S(1)}, u32[]{:S(2)}, u32[]{:S(2)}) async-start(bf16[8,136,128]{2,1,0:T(8,128)(2,1)} %bitcast_bitcast_fusion), calls=%async_computation.1 | async-start | bytes 557056 | tf_op jit(solution)/shard_map/all_to_all | solution.py:121
  168.4 104.5 %all-gather.17.cloned.1.call-start = ((), (), s32[]{:S(2)}) async-start(), calls=%async_computation.17 | async-start | bytes 2506752 | tf_op jit(solution)/shard_map/all_gather | solution.py:131
  242.2 63.2 %all-gather.19.cloned.1.call-start = ((), (), s32[]{:S(2)}) async-start(), calls=%async_computation.18 | async-start | bytes 2506752 | tf_op jit(solution)/shard_map/all_gather | solution.py:131
  243.1 100.5 %reduce-scatter.41.cloned.1.call-start = ((), (), s32[]{:S(2)}) async-start(), calls=%async_computation.29 | async-start | bytes 1740800
  311.0 32.7 %copy-start.21 = (f32[544,272]{0,1:T(8,128)S(1)}, f32[544,272]{0,1:T(8,128)}, u32[]{:S(2)}) copy-start(f32[544,272]{0,1:T(8,128)} %param.24) | copy-start | bytes 1775620
  313.6 62.7 %all-gather.23.cloned.1.call-start = ((), (), s32[]{:S(2)}) async-start(), calls=%async_computation.22 | async-start | bytes 1740800 | tf_op jit(solution)/shard_map/all_gather | solution.py:226
  346.8 81.1 %reduce-scatter.31.cloned.1.call-start = ((), (), s32[]{:S(2)}) async-start(), calls=%async_computation.24 | async-start | bytes 2654208
  376.3 6.9 copy-start.11
  390.8 75.4 %reduce-scatter.29.cloned.1.call-start = ((), (), s32[]{:S(2)}) async-start(), calls=%async_computation.23 | async-start | bytes 2654208
  400.6 126.4 %reduce-scatter.25.cloned.1.call-start = ((), (), s32[]{:S(2)}) async-start(), calls=%async_computation.19 | async-start | bytes 2506752 | tf_op jit(solution)/shard_map/reduce_scatter | solution.py:261
  489.0 76.0 %reduce-scatter.27.cloned.1.call-start = ((), (), s32[]{:S(2)}) async-start(), calls=%async_computation.20 | async-start | bytes 2506752 | tf_op jit(solution)/shard_map/reduce_scatter | solution.py:262
  489.6 156.0 %reduce-scatter.35.cloned.1.call-start = ((), (), s32[]{:S(2)}) async-start(), calls=%async_computation.26 | async-start | bytes 2820096
  492.2 198.9 %reduce-scatter.33.cloned.1.call-start = ((), (), s32[]{:S(2)}) async-start(), calls=%async_computation.25 | async-start | bytes 2654208
  574.6 160.1 %reduce-scatter.39.cloned.1.call-start = ((), (), s32[]{:S(2)}) async-start(), calls=%async_computation.28 | async-start | bytes 1566720
  638.0 7.2 copy-start.18
  639.6 43.8 %all-to-all-start.3 = ((bf16[8,136,408]{2,1,0:T(8,128)(2,1)}), bf16[8,136,408]{2,1,0:T(8,128)(2,1)S(1)}, u32[]{:S(2)}, u32[]{:S(2)}) async-start(bf16[8,136,408]{2,1,0:T(8,128)(2,1)} %bitcast.27), calls=%async_computation.5 | async-start | bytes 2228224 | tf_op jit(solution)/shard_map/all_to_all | solution.py:121
  643.2 112.0 %reduce-scatter.37.cloned.1.call-start = ((), (), s32[]{:S(2)}) async-start(), calls=%async_computation.27 | async-start | bytes 1566720
  691.2 30.4 %copy-start.2 = (bf16[136,4,816]{2,1,0:T(4,128)(2,1)S(1)}, bf16[136,4,816]{2,1,0:T(4,128)(2,1)}, u32[]{:S(2)}) copy-start(bf16[136,4,816]{2,1,0:T(4,128)(2,1)} %reshape.207) | copy-start | bytes 2663428
  692.5 29.1 %copy-start.8 = (bf16[128,1088]{0,1:T(8,128)(2,1)}, bf16[128,1088]{0,1:T(8,128)(2,1)S(1)}, u32[]{:S(2)}) copy-start(bf16[128,1088]{0,1:T(8,128)(2,1)S(1)} %copy.232) | copy-start | bytes 835588
  763.7 8.0 %copy-start.4 = (f32[136,816]{0,1:T(8,128)S(1)}, f32[136,816]{0,1:T(8,128)}, u32[]{:S(2)}) copy-start(f32[136,816]{0,1:T(8,128)} %get-tuple-element.190) | copy-start | bytes 1331716
  765.8 7.0 copy-start.17
  765.8 7.8 copy-start.3
  767.7 7.0 copy-start.16
  769.9 5.6 copy-start.26
  769.9 5.6 copy-start.27
  769.9 5.6 copy-start.28
  (20 other events, 57.8 us)
Sparse Core Ops, SparseCore 0:
  13.0 41.2 all-gather.20
  60.1 37.2 all-gather.12
  99.6 56.9 all-gather.10
  162.4 53.7 all-gather.14
  242.4 30.4 all-gather.16
  274.9 30.5 all-gather.18
  313.7 29.8 reduce-scatter.40
  347.0 29.3 all-gather.22
  390.9 37.0 reduce-scatter.30
  430.1 35.9 reduce-scatter.28
  489.1 37.8 reduce-scatter.24
  529.2 35.7 reduce-scatter.26
  567.3 46.5 reduce-scatter.34
  616.1 57.1 reduce-scatter.32
  676.1 38.8 reduce-scatter.38
  727.5 27.5 reduce-scatter.36

commit v2 on v1

--- a/solution.py
+++ b/solution.py
@@ -176,6 +176,7 @@
         ],
         axis=1,
     )
+    normed_one, inverse_one = layer_norm(stream)
     tw, mw, ew = triple_weight.shape[1], merge_weight.shape[1], expand_weight.shape[1]
     columns = lax.all_gather(packed, "dp", axis=0)
 
@@ -186,8 +187,12 @@
     merge_rows = take(tw, mw)
     expand_rows = take(tw + mw, ew)
     vector_rows = take(tw + mw + ew, vector_params.shape[1])
-    normed_one, inverse_one = layer_norm(stream)
-    normed_full = gather_rows(normed_one.astype(bf16))
+    normed_send, columns_done = lax.optimization_barrier((normed_one.astype(bf16), columns))
+    normed_full = gather_rows(normed_send)
+    vector_rows, normed_full = lax.optimization_barrier((vector_rows, normed_full))
+    vectors = gather_rows(vector_rows).astype(jnp.float32)
+    shrink_send, vectors = lax.optimization_barrier((shrink_weight.astype(bf16), vectors))
+    w_shrink = lax.all_gather(shrink_send, "dp", axis=0).transpose(1, 0, 2).reshape(wide, D)
     send = jnp.concatenate(
         [
             triple_rows.reshape(feat, 3, n, feat).transpose(2, 0, 1, 3).reshape(n, feat, 3 * feat),
@@ -198,9 +203,6 @@
     got = exchange(send).reshape(D, 3 * feat + wide)
     w_triple = got[:, : 3 * feat]
     w_expand = got[:, 3 * feat :]
-    merged = gather_rows(jnp.concatenate([merge_rows, vector_rows], axis=1))
-    w_merge = merged[:, :D]
-    vectors = merged[:, D:].astype(jnp.float32)
     gain_one = vectors[:, 0]
     shift_one = vectors[:, 1]
     query_bias = lax.dynamic_slice_in_dim(vectors[:, 2], here * feat, feat)
@@ -215,39 +217,40 @@
     bias = jnp.concatenate([query_bias, jnp.zeros_like(query_bias), value_bias])
     triple_t = (dot_on(w_triple, act_one, 0, 1) + bias[:, None]).astype(bf16)
     query_t = exchange(triple_t[:feat].reshape(feat, n, rows).transpose(1, 0, 2)).reshape(D, rows)
-    both = lax.all_gather(triple_t[feat:].reshape(2, feat, total), "ctx", axis=0)
+    pair_send, w_shrink = lax.optimization_barrier(
+        (triple_t[feat:].reshape(2, feat, total), w_shrink)
+    )
+    both = lax.all_gather(pair_send, "ctx", axis=0)
+    merge_rows, both = lax.optimization_barrier((merge_rows, both))
+    w_merge = gather_rows(merge_rows)
     key_t = both[:, 0].reshape(D, total)
     value_t = both[:, 1].reshape(D, total)
     (attended_t,) = attention(
         forward_kernel, query_pos, key_pos, (query_t, key_t, value_t), (rows,)
     )
-    cot_full = gather_rows(cotangent.astype(bf16))
-    w_shrink = (
-        lax.all_gather(shrink_weight.astype(bf16), "dp", axis=0).transpose(1, 0, 2).reshape(wide, D)
-    )
     middle = stream + dot_on(attended_t, w_merge, 0, 0) + merge_bias
     normed_two, inverse_two = layer_norm(middle)
     act_two = gather_rows((normed_two * gain_two + shift_two).astype(bf16))
+    cot_send, act_two = lax.optimization_barrier((cotangent.astype(bf16), act_two))
+    cot_full = gather_rows(cot_send)
     pre_act = dot_on(act_two, w_expand, 1, 0) + expand_bias
     hidden_b = gelu_value(pre_act).astype(bf16)
     dpre = dot_on(cot_full, w_shrink, 1, 1) * gelu_slope(pre_act)
     dpre_b = dpre.astype(bf16)
     expand_bias_grad = jnp.sum(dpre, axis=0)
     dact_two = scatter_rows(dot_on(dpre_b, w_expand, 1, 1))
-    block_out = middle + scatter_rows(dot_on(hidden_b, w_shrink, 1, 0)) + shrink_bias
+    out_part = dot_on(hidden_b, w_shrink, 1, 0).astype(bf16)
+    out_part, dact_two = lax.optimization_barrier((out_part, dact_two))
+    block_rows = scatter_rows(out_part)
+    block_out = middle + block_rows + shrink_bias
     shrink_part = dot_on(hidden_b, cot_full, 0, 0).astype(bf16)
     expand_part = dot_on(act_two, dpre_b, 0, 0).astype(bf16)
-    shrink_grad = lax.psum_scatter(
-        shrink_part.reshape(wide, m, D // m).transpose(1, 0, 2), "dp", scatter_dimension=0
-    ).astype(jnp.float32)
     shrink_bias_grad = jnp.sum(cotangent, axis=0)
     gain_two_grad = jnp.sum(dact_two * normed_two, axis=0)
     shift_two_grad = jnp.sum(dact_two, axis=0)
     dmiddle = cotangent + norm_back(dact_two, normed_two, inverse_two, gain_two)
     dmiddle_b = dmiddle.astype(bf16)
-    merge_part = lax.psum_scatter(
-        dot_on(attended_t, dmiddle_b, 1, 0).astype(bf16), "ctx", scatter_dimension=0, tiled=True
-    )
+    merge_part = dot_on(attended_t, dmiddle_b, 1, 0).astype(bf16)
     merge_bias_grad = jnp.sum(dmiddle, axis=0)
     dattended_t = dot_on(w_merge, dmiddle_b, 1, 1).astype(bf16)
     dquery_t, dkey_t, dvalue_t = attention(
@@ -265,6 +268,9 @@
     value_bias_grad = jnp.sum(dvalue_c.astype(jnp.float32), axis=1)
     dact_one = scatter_rows(dot_on(dtriple_t, w_triple, 0, 1))
     triple_part = dot_on(act_one, dtriple_t, 0, 1).astype(bf16)
+    shrink_part, expand_part, merge_part, triple_part, dact_one = lax.optimization_barrier(
+        (shrink_part, expand_part, merge_part, triple_part, dact_one)
+    )
     gain_one_grad = jnp.sum(dact_one * normed_one, axis=0)
     shift_one_grad = jnp.sum(dact_one, axis=0)
     input_rows = dmiddle + norm_back(dact_one, normed_one, inverse_one, gain_one)
@@ -294,29 +300,33 @@
         axis=1,
     )
     vector_part = lax.psum_scatter(vector_local, "ctx", scatter_dimension=0, tiled=True)
-
-    def by_dp(rows_part):
-        return rows_part.reshape(feat, m, -1).transpose(1, 0, 2)
-
-    expand_rows_part = exchange(expand_part.reshape(n, feat, wide)).transpose(1, 0, 2)
-    expand_grad = lax.psum_scatter(by_dp(expand_rows_part), "dp", scatter_dimension=0).astype(
-        jnp.float32
-    )
-    triple_rows_part = (
-        exchange(triple_part.reshape(n, feat, 3 * feat))
-        .reshape(n, feat, 3, feat)
-        .transpose(1, 2, 0, 3)
-    )
-    last = lax.psum_scatter(
-        jnp.concatenate(
-            [by_dp(triple_rows_part), by_dp(merge_part), by_dp(vector_part).astype(bf16)], axis=2
-        ),
-        "dp",
-        scatter_dimension=0,
+    vector_grad = lax.psum_scatter(vector_part, "dp", scatter_dimension=1, tiled=True)
+
+    def own_block(part, groups, width):
+        pieces = part.reshape(n, feat, groups, -1)
+        if feat % m:
+            spread = exchange(pieces).transpose(1, 2, 0, 3).reshape(feat, m, width)
+            return lax.psum_scatter(spread.transpose(1, 0, 2), "dp", scatter_dimension=0)
+        fine = feat // m
+        split = pieces.reshape(n, m, fine, groups, -1).transpose(1, 0, 2, 3, 4)
+        split = split.reshape(m, n, fine, -1)
+        summed = lax.psum_scatter(split, "dp", scatter_dimension=0)
+        spread = exchange(summed).reshape(n, fine, groups, -1).transpose(1, 2, 0, 3)
+        spread = spread.reshape(fine, m, width).transpose(1, 0, 2)
+        return lax.all_to_all(spread, "dp", split_axis=0, concat_axis=0, tiled=True).reshape(
+            feat, width
+        )
+
+    def sum_columns(part):
+        pieces = part.reshape(part.shape[0], m, -1).transpose(1, 0, 2)
+        return lax.psum_scatter(pieces, "dp", scatter_dimension=0)
+
+    shrink_grad = sum_columns(shrink_part).astype(jnp.float32)
+    merge_grad = lax.psum_scatter(
+        sum_columns(merge_part), "ctx", scatter_dimension=0, tiled=True
     ).astype(jnp.float32)
-    triple_grad = last[:, :tw]
-    merge_grad = last[:, tw : tw + mw]
-    vector_grad = last[:, tw + mw :]
+    expand_grad = own_block(expand_part, 1, ew).astype(jnp.float32)
+    triple_grad = own_block(triple_part, 3, tw).astype(jnp.float32)
     triple_new, triple_moment_new, triple_square_new = adam_update(
         triple_weight, triple_grad, triple_moment, triple_square, True
     )

time: 794 us -> 806 us (1.015)
  starting transfers between devices: 12.9 us -> 24.9 us
  blocking collectives: 93.1 us -> 104 us
    unnamed x23 -> x25, waiting for transfers between devices: 111 us -> 168 us
    all_gather x4, waiting for transfers between devices: 126 us -> 77.2 us  [gather_rows(): return lax.all_gather(rows, 'ctx', axis=0, tiled=True)]
    all_to_all x2 -> x1, blocking collectives: 65 us -> 16.2 us  [exchange(): lax.all_to_all(blocks, 'ctx', split_axis=0, concat_axis=0, tiled=True)]
    all_gather x0 -> x1, blocking collectives: none -> 43.3 us  [gather_rows(): return lax.all_gather(rows, 'ctx', axis=0, tiled=True)]
    unnamed x1 -> x2, blocking collectives: 28.1 us -> 44.2 us
    unnamed x93 -> x120, local copies, waits for them, and re-layouts: 44.4 us -> 29.3 us
    optimization_barrier x0 -> x4, local copies, waits for them, and re-layouts: none -> 10.9 us  [local(): lax.optimization_barrier((shrink_part, expand_part, merge_part, triple_pa...]
    another operation x0 -> x2, local copies, waits for them, and re-layouts: none -> 9.28 us  [own_block(): split = pieces.reshape(n, m, fine, groups, -1).transpose(1, 0, 2, 3, 4)]
  transfers between devices with their start and end apart: 19 -> 23, of which waited for: 15 -> 19; matrix products, arithmetic and copies ran while one was open for 14% -> 12% of each run, Pallas kernels for 0% -> 2%
where the time goes in v2:
time: 806 us; the launch traced here: 795 us
  waiting for transfers between devices  447 us (55%)
  blocking collectives  104 us (13%)
  local copies, waits for them, and re-layouts  101 us (13%)
  matrix products  41.6 us (5%)
  Pallas kernels  34.5 us (4%)
  other arithmetic  26.5 us (3%)
  starting transfers between devices  24.9 us (3%)
  between operations  16.4 us (2%)
    unnamed x25, waiting for transfers between devices  168 us
    all_gather x4, waiting for transfers between devices, gather_rows(): return lax.all_gather(rows, 'ctx', axis=0, tiled=True)  77.2 us
    all_gather x1, waiting for transfers between devices, local(): both = lax.all_gather(pair_send, 'ctx', axis=0)  48.6 us
    unnamed x2, blocking collectives  44.2 us
    all_gather x1, blocking collectives, gather_rows(): return lax.all_gather(rows, 'ctx', axis=0, tiled=True)  43.3 us
    dot_general x12, matrix products, dot_on(): lax.dot_general(left, right, (((left_dim,), (right_dim,)), ((), ())), pre...  41.6 us
    all_gather x1, waiting for transfers between devices, local(): columns = lax.all_gather(packed, 'dp', axis=0)  39.4 us
    reduce_scatter x1, waiting for transfers between devices, local(): lax.psum_scatter(dvalue_t, 'ctx', scatter_dimension=0, tiled=True)  36.9 us
  transfers between devices with their start and end apart: 23, of which 19 were waited for; matrix products, arithmetic and copies ran while one was open for 12% of the time, Pallas kernels for 2%

profile of v2, /device:TPU:0, one launch (start us, length us, event | category | flops | bytes accessed | tf_op | source)
XLA Modules:
  0.0 795.1 jit_solution(14410465120290566093)
XLA Ops:
  15.0 39.4 %all-gather.21.cloned.1.call-done = bf16[544,2179]{1,0:T(8,128)(2,1)} async-done(((bf16[136,2179]{1,0:T(8,128)(2,1)}), bf16[544,2179]{1,0:T(8,128)(2,1)}) %all-gather.21.cloned.1.call-update) | async-done | bytes 2370768 | tf_op jit(solution)/shard_map/all_gather | solution.py:181
  71.8 4.7 all-to-all-start
  78.5 18.4 %all-gather.13.cloned.1.call-done = bf16[1024,1088]{0,1:T(8,128)(2,1)} async-done(((bf16[128,1088]{0,1:T(8,128)(2,1)}), bf16[1024,1088]{0,1:T(8,128)(2,1)}) %all-gather.13.cloned.1.call-update) | async-done | bytes 2228240 | tf_op jit(solution)/shard_map/all_gather | solution.py:131
  96.8 43.3 %all-gather.3 = bf16[8,136,12]{1,2,0:T(8,128)(2,1)S(1)} all-gather(bf16[1,136,12]{1,2,0:T(8,128)(2,1)S(1)} %bitcast.168), channel_id=1, replica_groups=mesh['dp'=4,'ctx'=8] {'ctx'}, dimensions={0}, use_global_device_ids=true | all-gather | bytes 29376 | tf_op jit(solution)/shard_map/all_gather | solution.py:131
  146.9 23.4 %all-gather.25.cloned.1.call-done = bf16[4,544,272]{1,2,0:T(8,128)(2,1)} async-done(((bf16[1,544,272]{1,2,0:T(8,128)(2,1)}), bf16[4,544,272]{1,2,0:T(8,128)(2,1)}) %all-gather.25.cloned.1.call-update) | async-done | bytes 1183760 | tf_op jit(solution)/shard_map/all_gather | solution.py:195
  172.8 48.6 %all-gather.23.cloned.1.call-done = bf16[16,136,1024]{2,1,0:T(8,128)(2,1)} async-done(((bf16[2,136,1024]{2,1,0:T(8,128)(2,1)}), bf16[16,136,1024]{2,1,0:T(8,128)(2,1)}) %all-gather.23.cloned.1.call-update) | async-done | bytes 4456464 | tf_op jit(solution)/shard_map/all_gather | solution.py:223
  228.7 5.2 fusion.29
  233.9 8.3 %all-to-all-done.1 = bf16[8,136,128]{2,1,0:T(8,128)(2,1)S(1)} async-done(((bf16[8,136,128]{2,1,0:T(8,128)(2,1)}), bf16[8,136,128]{2,1,0:T(8,128)(2,1)S(1)}, u32[]{:S(2)}, u32[]{:S(2)}) %all-to-all-start.1) | async-done | bytes 278560 | tf_op jit(solution)/shard_map/all_to_all | solution.py:121
  242.9 16.2 %shard_map.345.out_ref = bf16[1088,128]{1,0:T(8,128)(2,1)} custom-call(s32[128,1]{1,0:T(8,128)} %copy.156.query_pos, s32[1,1024]{1,0:T(1,128)} %add.239.key_pos, bf16[1088,128]{1,0:T(8,128)(2,1)} %bitcast.150, bf16[1088,1024]{1,0:T(8,128)(2,1)} %bitcast.134, bf16[1088,1024]{1,0:T(8,128)(2,1)} %bitcast.132), custom_call_target="tpu_custom_call" | custom-call | flops 570425344 | bytes 8912896 | tf_op jit(solution)/shard_map/pallas_call | solution.py:108
  265.0 31.6 %all-gather.17.cloned.1.call-done = bf16[1024,1088]{0,1:T(8,128)(2,1)} async-done(((bf16[128,1088]{0,1:T(8,128)(2,1)}), bf16[1024,1088]{0,1:T(8,128)(2,1)}) %all-gather.17.cloned.1.call-update) | async-done | bytes 2228240 | tf_op jit(solution)/shard_map/all_gather | solution.py:131
  296.8 5.4 fusion.8
  302.2 27.1 %all-gather.19.cloned.1.call-done = bf16[1024,1088]{0,1:T(8,128)(2,1)} async-done(((bf16[128,1088]{0,1:T(8,128)(2,1)}), bf16[1024,1088]{0,1:T(8,128)(2,1)}) %all-gather.19.cloned.1.call-update) | async-done | bytes 2228240 | tf_op jit(solution)/shard_map/all_gather | solution.py:131
  329.3 5.7 fusion.32
  339.5 4.2 copy.174
  344.1 4.2 convolution_convert_fusion.2
  348.4 31.5 %reduce-scatter.30.cloned.1.call-done = bf16[128,1088]{1,0:T(8,128)(2,1)} async-done(((bf16[1024,1088]{1,0:T(8,128)(2,1)}), bf16[128,1088]{1,0:T(8,128)(2,1)}) %reduce-scatter.30.cloned.1.call-update) | async-done | bytes 278544
  386.5 34.1 %reduce-scatter.32.cloned.1.call-done = bf16[128,1088]{1,0:T(8,128)(2,1)} async-done(((bf16[1024,1088]{1,0:T(8,128)(2,1)}), bf16[128,1088]{1,0:T(8,128)(2,1)}) %reduce-scatter.32.cloned.1.call-update) | async-done | bytes 278544
  426.7 18.3 %shard_map.346 = (bf16[1088,128]{1,0:T(8,128)(2,1)}, bf16[1088,1024]{1,0:T(8,128)(2,1)}, bf16[1088,1024]{1,0:T(8,128)(2,1)}) custom-call(s32[128,1]{1,0:T(8,128)} %copy.156.query_pos, s32[1,1024]{1,0:T(1,128)} %add.239.key_pos, bf16[1088,128]{1,0:T(8,128)(2,1)} %bitcast.151, bf16[1088,1024]{1,0:T(8,128)(2,1)} %bitcast.135, bf16[1088,1024]{1,0:T(8,128)(2,1)} %bitcast.133, ...), custom_call_target="tpu_custom_call" | custom-call | flops 1426063360 | bytes 8912896 | tf_op jit(solution)/shard_map/pallas_call | solution.py:108
  445.9 16.2 %all_to_all.35 = bf16[8,136,128]{2,1,0:T(8,128)(2,1)S(1)} all-to-all(bf16[8,136,128]{2,1,0:T(8,128)(2,1)S(1)} %bitcast.166), channel_id=1, replica_groups=mesh['dp'=4,'ctx'=8] {'ctx'}, dimensions={0} | all-to-all | bytes 557056 | tf_op jit(solution)/shard_map/all_to_all | solution.py:121
  462.8 20.6 %reduce-scatter.26.cloned.1.call-done = bf16[136,1024]{1,0:T(8,128)(2,1)} async-done(((bf16[1088,1024]{1,0:T(8,128)(2,1)}), bf16[136,1024]{1,0:T(8,128)(2,1)}) %reduce-scatter.26.cloned.1.call-update) | async-done | bytes 278544 | tf_op jit(solution)/shard_map/reduce_scatter | solution.py:264
  485.1 36.9 %reduce-scatter.28.cloned.1.call-done = bf16[136,1024]{1,0:T(8,128)(2,1)} async-done(((bf16[1088,1024]{1,0:T(8,128)(2,1)}), bf16[136,1024]{1,0:T(8,128)(2,1)}) %reduce-scatter.28.cloned.1.call-update) | async-done | bytes 278544 | tf_op jit(solution)/shard_map/reduce_scatter | solution.py:265
  545.1 22.6 %reduce-scatter.34.cloned.1.call-done = bf16[128,1088]{1,0:T(8,128)(2,1)} async-done(((bf16[1024,1088]{1,0:T(8,128)(2,1)}), bf16[128,1088]{1,0:T(8,128)(2,1)}) %reduce-scatter.34.cloned.1.call-update) | async-done | bytes 278544
  573.7 5.8 reshape_reshape.14
  579.5 5.3 reshape.233
  607.8 7.2 reduce-scatter.36.cloned.1.call-done
  616.8 4.8 all-to-all-start.3
  622.7 10.0 %all-to-all-done.3 = bf16[8,34,408]{2,1,0:T(8,128)(2,1)S(1)} async-done(((bf16[8,34,408]{2,1,0:T(8,128)(2,1)}), bf16[8,34,408]{2,1,0:T(8,128)(2,1)S(1)}, u32[]{:S(2)}, u32[]{:S(2)}) %all-to-all-start.3) | async-done | bytes 221984 | tf_op jit(solution)/shard_map/all_to_all | solution.py:121
  638.0 27.7 %all-reduce.5 = f32[1088,12]{0,1:T(8,128)S(1)} all-reduce(f32[1088,12]{0,1:T(8,128)S(1)} %concatenate.19), channel_id=15, replica_groups=mesh['dp'=4,'ctx'=8] {'ctx'}, use_global_device_ids=true, to_apply=%region_27.0.clone | all-reduce | flops 13056 | bytes 104448
  665.8 16.5 %all-reduce.6 = f32[136,12]{0,1:T(8,128)S(1)} all-reduce(f32[136,12]{0,1:T(8,128)S(1)} %constant_dynamic-slice_fusion.1), channel_id=16, replica_groups=mesh['dp'=4,'ctx'=8] {'dp'}, use_global_device_ids=true, to_apply=%region_28.0.clone | all-reduce | flops 1632 | bytes 13056
  689.7 10.6 %all-to-all-done.5 = bf16[8,34,544]{2,1,0:T(8,128)(2,1)S(1)} async-done(((bf16[8,34,544]{2,1,0:T(8,128)(2,1)}), bf16[8,34,544]{2,1,0:T(8,128)(2,1)S(1)}, u32[]{:S(2)}, u32[]{:S(2)}) %all-to-all-start.5) | async-done | bytes 295968 | tf_op jit(solution)/shard_map/all_to_all | solution.py:121
  711.9 15.8 %reduce-scatter.38.cloned.1.call-done = bf16[1,1088,272]{1,2,0:T(8,128)(2,1)} async-done(((bf16[4,1088,272]{1,2,0:T(8,128)(2,1)}), bf16[1,1088,272]{1,2,0:T(8,128)(2,1)}) %reduce-scatter.38.cloned.1.call-update) | async-done | bytes 591888
  730.7 55.5 %all-reduce.9.cloned.1.call-done = bf16[1088,272]{0,1:T(8,128)(2,1)} async-done(((bf16[1088,272]{0,1:T(8,128)(2,1)}), bf16[1088,272]{0,1:T(8,128)(2,1)}) %all-reduce.9.cloned.1.call-update) | async-done | bytes 591888
  (272 shorter events, 153.4 us)
Async XLA Ops:
  7.2 47.2 %all-gather.21.cloned.1.call-start = ((), (), s32[]{:S(2)}) async-start(), calls=%async_computation.22 | async-start | bytes 3133440 | tf_op jit(solution)/shard_map/all_gather | solution.py:181
  12.9 83.9 %all-gather.13.cloned.1.call-start = ((), (), s32[]{:S(2)}) async-start(), calls=%async_computation.16 | async-start | bytes 2506752 | tf_op jit(solution)/shard_map/all_gather | solution.py:131
  71.8 69.3 %all-to-all-start = ((bf16[8,136,952]{2,1,0:T(8,128)(2,1)}), bf16[8,136,952]{2,1,0:T(8,128)(2,1)S(1)}, u32[]{:S(2)}, u32[]{:S(2)}) async-start(bf16[8,136,952]{2,1,0:T(8,128)(2,1)} %copy.151), calls=%async_computation | async-start | bytes 4456448 | tf_op jit(solution)/shard_map/all_to_all | solution.py:121
  76.6 93.7 %all-gather.25.cloned.1.call-start = ((), (), s32[]{:S(2)}) async-start(), calls=%async_computation.24 | async-start | bytes 1740800 | tf_op jit(solution)/shard_map/all_gather | solution.py:195
  140.3 81.1 %all-gather.23.cloned.1.call-start = ((), (), s32[]{:S(2)}) async-start(), calls=%async_computation.23 | async-start | bytes 5013504 | tf_op jit(solution)/shard_map/all_gather | solution.py:223
  146.0 75.4 %copy-start.44 = (s32[8,2]{0,1:T(2,128)S(1)}, s32[8,2]{0,1:T(2,128)}, u32[]{:S(2)}) copy-start(s32[8,2]{0,1:T(2,128)} %param.20) | copy-start | bytes 196
  170.3 89.0 %all-gather.15.cloned.1.call-start = ((), (), s32[]{:S(2)}) async-start(), calls=%async_computation.17 | async-start | bytes 2820096 | tf_op jit(solution)/shard_map/all_gather | solution.py:131
  224.1 18.0 %all-to-all-start.1 = ((bf16[8,136,128]{2,1,0:T(8,128)(2,1)}), bf16[8,136,128]{2,1,0:T(8,128)(2,1)S(1)}, u32[]{:S(2)}, u32[]{:S(2)}) async-start(bf16[8,136,128]{2,1,0:T(8,128)(2,1)} %bitcast_bitcast_fusion), calls=%async_computation.1 | async-start | bytes 557056 | tf_op jit(solution)/shard_map/all_to_all | solution.py:121
  227.6 69.0 %all-gather.17.cloned.1.call-start = ((), (), s32[]{:S(2)}) async-start(), calls=%async_computation.18 | async-start | bytes 2506752 | tf_op jit(solution)/shard_map/all_gather | solution.py:131
  264.2 65.2 %all-gather.19.cloned.1.call-start = ((), (), s32[]{:S(2)}) async-start(), calls=%async_computation.19 | async-start | bytes 2506752 | tf_op jit(solution)/shard_map/all_gather | solution.py:131
  296.6 83.3 %reduce-scatter.30.cloned.1.call-start = ((), (), s32[]{:S(2)}) async-start(), calls=%async_computation.25 | async-start | bytes 2654208
  343.7 76.9 %reduce-scatter.32.cloned.1.call-start = ((), (), s32[]{:S(2)}) async-start(), calls=%async_computation.26 | async-start | bytes 2654208
  384.5 98.9 %reduce-scatter.26.cloned.1.call-start = ((), (), s32[]{:S(2)}) async-start(), calls=%async_computation.20 | async-start | bytes 2506752 | tf_op jit(solution)/shard_map/reduce_scatter | solution.py:264
  445.0 77.1 %reduce-scatter.28.cloned.1.call-start = ((), (), s32[]{:S(2)}) async-start(), calls=%async_computation.21 | async-start | bytes 2506752 | tf_op jit(solution)/shard_map/reduce_scatter | solution.py:265
  445.0 78.7 %copy-start.16 = (bf16[8,136,952]{2,1,0:T(8,128)(2,1)S(1)}, bf16[8,136,952]{2,1,0:T(8,128)(2,1)}, u32[]{:S(2)}) copy-start(bf16[8,136,952]{2,1,0:T(8,128)(2,1)} %copy-done.14) | copy-start | bytes 6214660
  445.7 122.0 %reduce-scatter.34.cloned.1.call-start = ((), (), s32[]{:S(2)}) async-start(), calls=%async_computation.27 | async-start | bytes 2654208
  531.8 83.3 %reduce-scatter.36.cloned.1.call-start = ((), (), s32[]{:S(2)}) async-start(), calls=%async_computation.29 | async-start | bytes 1392640
  587.7 94.5 %reduce-scatter.40.cloned.1.call-start = ((), (), s32[]{:S(2)}) async-start(), calls=%async_computation.31 | async-start | bytes 1740800
  596.8 108.1 %reduce-scatter.42.cloned.1.call-start = ((), (), s32[]{:S(2)}) async-start(), calls=%async_computation.32 | async-start | bytes 1740800
  599.5 128.2 %reduce-scatter.38.cloned.1.call-start = ((), (), s32[]{:S(2)}) async-start(), calls=%async_computation.30 | async-start | bytes 3133440
  616.8 15.9 %all-to-all-start.3 = ((bf16[8,34,408]{2,1,0:T(8,128)(2,1)}), bf16[8,34,408]{2,1,0:T(8,128)(2,1)S(1)}, u32[]{:S(2)}, u32[]{:S(2)}) async-start(bf16[8,34,408]{2,1,0:T(8,128)(2,1)} %copy.161), calls=%async_computation.5 | async-start | bytes 655360 | tf_op jit(solution)/shard_map/all_to_all | solution.py:121
  633.2 54.4 %copy-start.35 = (f32[136,3]{0,1:T(4,128)S(1)}, f32[136,3]{0,1:T(4,128)}, u32[]{:S(2)}) copy-start(f32[136,3]{0,1:T(4,128)} %param.25) | copy-start | bytes 4900
  633.3 55.0 %copy-start.18 = (f32[136,816]{1,0:T(8,128)S(1)}, f32[136,816]{1,0:T(8,128)}, u32[]{:S(2)}) copy-start(f32[136,816]{1,0:T(8,128)} %param.21) | copy-start | bytes 1331716
  633.3 55.0 %copy-start.24 = (f32[136,816]{1,0:T(8,128)S(1)}, f32[136,816]{1,0:T(8,128)}, u32[]{:S(2)}) copy-start(f32[136,816]{1,0:T(8,128)} %param.26) | copy-start | bytes 1331716
  633.3 55.0 %copy-start.25 = (f32[136,816]{1,0:T(8,128)S(1)}, f32[136,816]{1,0:T(8,128)}, u32[]{:S(2)}) copy-start(f32[136,816]{1,0:T(8,128)} %param.31) | copy-start | bytes 1331716
  634.6 49.5 %all-to-all-start.4 = ((bf16[4,34,816]{2,1,0:T(8,128)(2,1)}), bf16[4,34,816]{2,1,0:T(8,128)(2,1)S(1)}, u32[]{:S(2)}, u32[]{:S(2)}) async-start(bf16[4,34,816]{2,1,0:T(8,128)(2,1)} %copy.164), calls=%async_computation.6 | async-start | bytes 573440 | tf_op jit(solution)/shard_map/all_to_all | solution.py:316
  684.1 16.3 %all-to-all-start.5 = ((bf16[8,34,544]{2,1,0:T(8,128)(2,1)}), bf16[8,34,544]{2,1,0:T(8,128)(2,1)S(1)}, u32[]{:S(2)}, u32[]{:S(2)}) async-start(bf16[8,34,544]{2,1,0:T(8,128)(2,1)} %copy.169), calls=%async_computation.7 | async-start | bytes 819200 | tf_op jit(solution)/shard_map/all_to_all | solution.py:121
  701.4 10.3 %all-to-all-start.6 = ((bf16[4,34,1088]{2,1,0:T(8,128)(2,1)}), bf16[4,34,1088]{2,1,0:T(8,128)(2,1)S(1)}, u32[]{:S(2)}, u32[]{:S(2)}) async-start(bf16[4,34,1088]{2,1,0:T(8,128)(2,1)} %copy.171), calls=%async_computation.8 | async-start | bytes 737280 | tf_op jit(solution)/shard_map/all_to_all | solution.py:316
  704.9 81.2 %all-reduce.9.cloned.1.call-start = ((), (), s32[]{:S(2)}) async-start(), calls=%async_computation.28 | async-start | bytes 1253376
  727.8 59.6 %copy-start.21 = (f32[136,272]{1,0:T(8,128)S(1)}, f32[136,272]{1,0:T(8,128)}, u32[]{:S(2)}) copy-start(f32[136,272]{1,0:T(8,128)} %param.22) | copy-start | bytes 443908
  727.8 59.6 %copy-start.27 = (f32[136,272]{1,0:T(8,128)S(1)}, f32[136,272]{1,0:T(8,128)}, u32[]{:S(2)}) copy-start(f32[136,272]{1,0:T(8,128)} %param.27) | copy-start | bytes 443908
  727.8 59.6 %copy-start.28 = (f32[136,272]{1,0:T(8,128)S(1)}, f32[136,272]{1,0:T(8,128)}, u32[]{:S(2)}) copy-start(f32[136,272]{1,0:T(8,128)} %param.32) | copy-start | bytes 443908
  (43 other events, 409.3 us)
Sparse Core Ops, SparseCore 0:
  13.1 41.2 all-gather.20
  56.6 40.2 all-gather.12
  140.4 29.8 all-gather.24
  172.3 49.0 all-gather.22
  223.5 35.7 all-gather.14
  264.3 32.2 all-gather.16
  298.7 30.5 all-gather.18
  343.8 36.0 reduce-scatter.29
  384.6 35.9 reduce-scatter.31
  445.1 38.2 reduce-scatter.25
  485.7 36.2 reduce-scatter.27
  531.9 35.7 reduce-scatter.33
  587.9 27.1 reduce-scatter.35
  618.0 30.9 reduce-scatter.39
  651.8 31.1 reduce-scatter.41
  685.9 41.8 reduce-scatter.37
  729.9 56.1 all-reduce.8
